TPU v7x, 512 devices: a whole 4x8x8 slice. The times are simulated.
512 devices in a mesh: rows: 128 (over z, y_hi, x), feat: 4 (over y_lo, core).
Axes of the slice: x: 4, y: 8 (y_hi: 4, y_lo: 2; y = y_hi * 2 + y_lo), z: 8, core: 2. Of those that a mesh axis runs over, the one named last changes fastest.
Arguments:
- band_feats: float32 [65536, 1024], P('rows', 'feat'), may hold values from -6 to 6
- head_feats: float32 [512, 1024], P('rows', 'feat'), may hold values from -6 to 6
- mix_weights: bfloat16 [2, 1024, 1024], P(None, None, 'feat'), may hold values from -0.1875 to 0.1875
- tile_place: int32 [4096, 3], P('rows'), may hold values from -1 to 3, as said below
- tile_vals: bfloat16 [4096, 128, 128], P('rows'), may hold values from -1 to 1
- arrow_cols: bfloat16 [65536, 512], P('rows'), may hold values from -1 to 1
- arrow_reach: int32 [65536], P('rows'), may hold values from 1 to 512
- arrow_rows: bfloat16 [512, 65536], P(None, 'rows'), may hold values from -0.125 to 0.125
- band_degree: int32 [65536], P('rows'), may hold values from 8 to 32
- head_degree: int32 [512], replicated, may hold values from 8 to 32
Outputs:
- band_out: float32 [65536, 1024], P('rows', 'feat')
- head_out: float32 [512, 1024], P('rows', 'feat')
Inputs may be any that keep to these rules, and one draw needn't show every extreme that they name: `tile_place`: row and column lie in 0 to 3 and the offset in -1 to 1; the 32 slots of every block hold offsets -1, 0 and 1.
All inputs are finite; a program needn't handle non-finite values.
Results may differ from a plain program's by a relative error of at most 0.0057.
Values may be sent and summed in bfloat16 or wider, within the bound.
A program may use at most 64 MiB of HBM per device.

v0:
```python
import jax
import jax.numpy as jnp
from jax import lax
from jax.sharding import Mesh
from jax.sharding import PartitionSpec as P

ROWS = ("rows_0", "rows_1", "rows_2")


def side_by_side(arrays, axis, dim, along):
    both = jnp.concatenate(arrays, axis=along)
    result, at, gathered = (lax.all_gather(both, axis, axis=dim, tiled=True), 0, [])
    for a in arrays:
        gathered.append(lax.slice_in_dim(result, at, at + a.shape[along], axis=along))
        at += a.shape[along]
    return tuple(gathered)


def sent_to_all(shard, axis):
    copies = jnp.broadcast_to(shard, (lax.axis_size(axis), *shard.shape))
    return lax.all_to_all(copies, axis, split_axis=0, concat_axis=0, tiled=True)


def laid_out(parts, dim):
    dims = list(parts.shape[1:])
    dims[dim] *= parts.shape[0]
    return jnp.moveaxis(parts, 0, dim).reshape(dims)


def gathered_by_axis(shard, axes, dim):
    far, near = axes
    parts = sent_to_all(sent_to_all(shard, far), near)
    return laid_out(parts.swapaxes(0, 1).reshape(-1, *shard.shape), dim)


def extended(cells, sides, width):
    for axis, dim in sides:
        count = lax.axis_size(axis)
        ends = count - 1
        head = lax.slice_in_dim(cells, 0, width, axis=dim)
        tail = lax.slice_in_dim(cells, cells.shape[dim] - width, cells.shape[dim], axis=dim)
        cells = jnp.concatenate(
            [
                lax.ppermute(tail, axis, [(i, (i + 1) % count) for i in range(ends)]),
                cells,
                lax.ppermute(head, axis, [((i + 1) % count, i) for i in range(ends)]),
            ],
            axis=dim,
        )
    return cells


def in_blocks(shard, dim, size):
    before, after = (shard.shape[:dim], shard.shape[dim + 1 :])
    return jnp.moveaxis(shard.reshape(*before, size, -1, *after), dim, 0)


def sent_and_summed(shard, axis, dim):
    size = lax.axis_size(axis)
    parts = lax.all_to_all(in_blocks(shard, dim, size), axis, 0, 0, tiled=True)
    return jnp.sum(parts, axis=0)


def sum_in_two_steps(shard, axes, dim):
    far, near = axes
    own = sent_and_summed(in_blocks(shard, dim, lax.axis_size(far)), near, dim + 1)
    return jnp.sum(lax.all_to_all(own, far, 0, 0, tiled=True), axis=0)


def rows_for(lines, size):
    spare = -lines.shape[0] % size
    if not spare:
        return lines
    return jnp.concatenate([lines, jnp.zeros((spare, *lines.shape[1:]), lines.dtype)])


def total_of(shard, axes):
    lines = shard.reshape(-1, shard.shape[-1])
    own = sum_in_two_steps(
        rows_for(lines, lax.axis_size(axes[0]) * lax.axis_size(axes[1])), axes, 0
    )
    whole = gathered_by_axis(own, axes, 0)
    return whole[: len(lines)].reshape(shard.shape)


def body(
    band_feats,
    head_feats,
    mix_weights,
    tile_place,
    tile_vals,
    arrow_cols,
    arrow_reach,
    arrow_rows,
    band_degree,
    head_degree,
):
    rows_dev = band_feats.shape[0]
    head_dev = head_feats.shape[0]
    tile_size = tile_vals.shape[1]
    tile_rows = rows_dev // tile_size
    arrow_width = arrow_cols.shape[1]
    feat_dev = band_feats.shape[1]
    position = lax.axis_index(ROWS)
    reach_mask = lax.broadcasted_iota(jnp.int32, (rows_dev, arrow_width), 1) < arrow_reach[:, None]
    masked_cols = jnp.where(reach_mask, arrow_cols, jnp.zeros_like(arrow_cols))
    window_col = (tile_place[:, 2] + 1) * tile_rows + tile_place[:, 1]
    row_onehot = (
        tile_place[:, 0][None, :] == lax.broadcasted_iota(jnp.int32, (tile_rows, 1), 0)
    ).astype(jnp.float32)
    band_scale = lax.rsqrt(band_degree.astype(jnp.float32))[:, None]
    head_scale_all = lax.rsqrt(head_degree.astype(jnp.float32))[:, None]
    own_head_scale = lax.dynamic_slice_in_dim(head_scale_all, position * head_dev, head_dev, 0)
    band_state, head_state = (band_feats, head_feats)
    for layer_step in range(mix_weights.shape[0]):
        mixing = mix_weights[layer_step]
        zero_init = (
            jnp.zeros((rows_dev, feat_dev), jnp.float32),
            jnp.zeros((head_dev, feat_dev), jnp.float32),
        )

        def transform(totals, pieces, start, mixing=mixing):
            return (
                jnp.dot(pieces[0], mixing, preferred_element_type=jnp.float32),
                jnp.dot(pieces[1], mixing, preferred_element_type=jnp.float32),
            )

        band_x, head_x = transform(
            zero_init,
            side_by_side(
                (band_state.astype(jnp.bfloat16), head_state.astype(jnp.bfloat16)), "feat", 1, 0
            ),
            jnp.int32(0),
        )
        band_x = band_x.astype(jnp.bfloat16)
        head_x = head_x.astype(jnp.bfloat16)
        whole_head = gathered_by_axis(head_x, (("rows_0", "rows_1"), "rows_2"), 0)
        window = extended(band_x, ((ROWS, 0),), rows_dev)
        picked = window.reshape(3 * tile_rows, tile_size, feat_dev)[window_col]
        products = jnp.einsum("sij,sjf->sif", tile_vals, picked, preferred_element_type=jnp.float32)
        band_sum = jnp.einsum(
            "rs,sif->rif", row_onehot, products, precision=lax.Precision.HIGHEST
        ).reshape(rows_dev, feat_dev)
        band_sum = band_sum + jnp.dot(masked_cols, whole_head, preferred_element_type=jnp.float32)
        head_part = jnp.dot(arrow_rows, band_x, preferred_element_type=jnp.float32)
        head_total = total_of(head_part, (("rows_0", "rows_1"), "rows_2"))
        head_sum = lax.dynamic_slice_in_dim(head_total, position * head_dev, head_dev, 0)
        band_state = jnp.maximum(band_sum * band_scale, 0.0)
        head_state = jnp.maximum(head_sum * own_head_scale, 0.0)
    return (band_state, head_state)


def solution(mesh):
    split = Mesh(
        mesh.devices.reshape(8, 4, 4, mesh.shape["feat"]), ("rows_0", "rows_1", "rows_2", "feat")
    )
    return jax.shard_map(
        body,
        mesh=split,
        in_specs=(
            P(ROWS, "feat"),
            P(ROWS, "feat"),
            P(None, None, "feat"),
            P(ROWS, None),
            P(ROWS, None, None),
            P(ROWS, None),
            P(ROWS),
            P(None, ROWS),
            P(ROWS),
            P(),
        ),
        out_specs=(P(ROWS, "feat"), P(ROWS, "feat")),
        check_vma=False,
    )
```

profile of v0, /device:TPU:1, one launch (start us, length us, event | category | flops | bytes accessed | tf_op | source)
XLA Modules:
  0.0 277.4 jit_solution(6107868502429181857)
XLA Ops:
  8.0 1.1 convert_element_type.31
  9.9 32.5 %all-gather.3.cloned.1.call-done = bf16[516,1024]{1,0:T(8,128)(2,1)} async-done(((bf16[516,256]{1,0:T(8,128)(2,1)}), bf16[516,1024]{1,0:T(8,128)(2,1)}) %all-gather.3.cloned.1.call-update) | async-done | bytes 1056784 | tf_op jit(solution)/shard_map/all_gather | solution.py:12
  42.4 1.8 convolution_convert_fusion.1
  45.0 0.8 copy.62
  45.8 4.3 %all-to-all-start.2 = ((f32[4,32,4,256]{3,2,1,0:T(4,128)}), f32[4,32,4,256]{3,2,1,0:T(4,128)S(1)}, u32[]{:S(2)}, u32[]{:S(2)}) async-start(f32[4,32,4,256]{3,2,1,0:T(4,128)} %copy.62), calls=%async_computation.2 | async-start | bytes 1048576 | tf_op jit(solution)/shard_map/all_to_all | solution.py:60
  50.1 1.2 convolution_convert_fusion.3
  51.4 8.3 %all-to-all-done.2 = f32[4,32,4,256]{3,2,1,0:T(4,128)S(1)} async-done(((f32[4,32,4,256]{3,2,1,0:T(4,128)}), f32[4,32,4,256]{3,2,1,0:T(4,128)S(1)}, u32[]{:S(2)}, u32[]{:S(2)}) %all-to-all-start.2) | async-done | bytes 524320 | tf_op jit(solution)/shard_map/all_to_all | solution.py:60
  60.3 12.4 %all-to-all-start = ((bf16[32,4,256]{2,1,0:T(4,128)(2,1)}), bf16[32,4,256]{2,1,0:T(4,128)(2,1)S(1)}, u32[]{:S(2)}, u32[]{:S(2)}) async-start(bf16[32,4,256]{2,1,0:T(4,128)(2,1)} %broadcast_in_dim.33), calls=%async_computation | async-start | bytes 131072 | tf_op jit(solution)/shard_map/all_to_all | solution.py:21
  72.7 1.3 collective-permute-start.1
  74.0 4.7 %collective-permute-start = (bf16[512,256]{1,0:T(8,128)(2,1)S(1)}, bf16[512,256]{1,0:T(8,128)(2,1)}, u32[]{:S(2)}, u32[]{:S(2)}) collective-permute-start(bf16[512,256]{1,0:T(8,128)(2,1)S(1)} %convolution_convert_fusion.1), channel_id=1, source_target_pairs={{0,4},{4,8},{8,12},{12,16},{16,20},{20,24},{24,28},{28,32},{32,36}... | collective-permute-start | bytes 786440 | tf_op jit(solution)/shard_map/ppermute | solution.py:44
  79.4 4.4 %all-to-all-done = bf16[32,4,256]{2,1,0:T(4,128)(2,1)S(1)} async-done(((bf16[32,4,256]{2,1,0:T(4,128)(2,1)}), bf16[32,4,256]{2,1,0:T(4,128)(2,1)S(1)}, u32[]{:S(2)}, u32[]{:S(2)}) %all-to-all-start) | async-done | bytes 65568 | tf_op jit(solution)/shard_map/all_to_all | solution.py:21
  83.8 6.5 %all-to-all-start.3 = ((f32[32,4,256]{2,1,0:T(4,128)}), f32[32,4,256]{2,1,0:T(4,128)S(1)}, u32[]{:S(2)}, u32[]{:S(2)}) async-start(f32[32,4,256]{2,1,0:T(4,128)} %reduce_sum.36), calls=%async_computation.3 | async-start | bytes 262144 | tf_op jit(solution)/shard_map/all_to_all | solution.py:67
  90.5 11.2 %all-to-all-done.3 = f32[32,4,256]{2,1,0:T(4,128)S(1)} async-done(((f32[32,4,256]{2,1,0:T(4,128)}), f32[32,4,256]{2,1,0:T(4,128)S(1)}, u32[]{:S(2)}, u32[]{:S(2)}) %all-to-all-start.3) | async-done | bytes 131104 | tf_op jit(solution)/shard_map/all_to_all | solution.py:67
  102.5 5.5 %all-to-all-start.1 = ((bf16[4,32,4,256]{3,2,1,0:T(4,128)(2,1)}), bf16[4,32,4,256]{3,2,1,0:T(4,128)(2,1)S(1)}, u32[]{:S(2)}, u32[]{:S(2)}) async-start(bf16[4,32,4,256]{3,2,1,0:T(4,128)(2,1)} %broadcast_in_dim.34), calls=%async_computation.1 | async-start | bytes 524288 | tf_op jit(solution)/shard_map/all_to_all | solution.py:21
  108.0 1.0 pad_maximum_fusion
  109.0 2.0 gather_fusion
  111.1 2.4 all-to-all-done.1
  114.2 4.3 %all-to-all-start.4 = ((f32[32,4,256]{2,1,0:T(4,128)}), f32[32,4,256]{2,1,0:T(4,128)S(1)}, u32[]{:S(2)}, u32[]{:S(2)}) async-start(f32[32,4,256]{2,1,0:T(4,128)} %broadcast_in_dim.35), calls=%async_computation.4 | async-start | bytes 262144 | tf_op jit(solution)/shard_map/all_to_all | solution.py:21
  118.5 4.3 %convolution_bitcast_fusion.1 = f32[32,128,256]{1,2,0:T(8,128)} fusion(bf16[32,128,256]{2,1,0:T(8,128)(2,1)} %gather_fusion, bf16[32,128,128]{2,1,0:T(8,128)(2,1)S(1)} %copy-done), kind=kOutput, calls=%fused_computation.3 | convolution fusion | flops 268435456 | bytes 7340032 | tf_op jit(solution)/shard_map/sij,sjf->sif/dot_general | solution.py:140
  122.8 5.5 %copy.58 = f32[32,128,256]{2,0,1:T(8,128)} copy(f32[32,128,256]{1,2,0:T(8,128)} %convolution_bitcast_fusion.1) | data formatting | bytes 8388608 | tf_op jit(solution)/shard_map/sij,sjf->sif/dot_general | solution.py:140
  128.3 1.4 all-to-all-done.4
  129.7 0.9 broadcast_in_dim.36
  130.5 3.5 %all-to-all-start.5 = ((f32[4,32,4,256]{3,2,1,0:T(4,128)}), f32[4,32,4,256]{3,2,1,0:T(4,128)S(1)}, u32[]{:S(2)}, u32[]{:S(2)}) async-start(f32[4,32,4,256]{3,2,1,0:T(4,128)} %broadcast_in_dim.36), calls=%async_computation.5 | async-start | bytes 1048576 | tf_op jit(solution)/shard_map/all_to_all | solution.py:21
  134.1 3.6 %fusion.23 = f32[4,128,256]{2,0,1:T(4,128)S(1)} fusion(f32[32,128,256]{2,0,1:T(8,128)} %copy.58, s32[32]{0:T(128)S(1)} %get-tuple-element.2), kind=kOutput, calls=%fused_computation.44 | convolution fusion | flops 50331776 | bytes 4718720 | tf_op jit(solution)/shard_map/rs,sif->rif/dot_general | solution.py:141
  138.4 1.4 fusion.4
  139.8 1.2 all-to-all-done.5
  142.0 29.3 %all-gather.5.cloned.1.call-done = bf16[516,1024]{1,0:T(8,128)(2,1)} async-done(((bf16[516,256]{1,0:T(8,128)(2,1)}), bf16[516,1024]{1,0:T(8,128)(2,1)}) %all-gather.5.cloned.1.call-update) | async-done | bytes 1056784 | tf_op jit(solution)/shard_map/all_gather | solution.py:12
  171.3 1.8 convolution_convert_fusion
  174.7 4.3 %all-to-all-start.8 = ((f32[4,32,4,256]{3,2,1,0:T(4,128)}), f32[4,32,4,256]{3,2,1,0:T(4,128)S(1)}, u32[]{:S(2)}, u32[]{:S(2)}) async-start(f32[4,32,4,256]{3,2,1,0:T(4,128)} %copy.70), calls=%async_computation.8 | async-start | bytes 1048576 | tf_op jit(solution)/shard_map/all_to_all | solution.py:60
  179.0 0.9 convolution_convert_fusion.2
  179.9 8.6 %all-to-all-done.8 = f32[4,32,4,256]{3,2,1,0:T(4,128)S(1)} async-done(((f32[4,32,4,256]{3,2,1,0:T(4,128)}), f32[4,32,4,256]{3,2,1,0:T(4,128)S(1)}, u32[]{:S(2)}, u32[]{:S(2)}) %all-to-all-start.8) | async-done | bytes 524320 | tf_op jit(solution)/shard_map/all_to_all | solution.py:60
  189.1 12.4 %all-to-all-start.6 = ((bf16[32,4,256]{2,1,0:T(4,128)(2,1)}), bf16[32,4,256]{2,1,0:T(4,128)(2,1)S(1)}, u32[]{:S(2)}, u32[]{:S(2)}) async-start(bf16[32,4,256]{2,1,0:T(4,128)(2,1)} %broadcast_in_dim.37), calls=%async_computation.6 | async-start | bytes 131072 | tf_op jit(solution)/shard_map/all_to_all | solution.py:21
  201.5 1.3 collective-permute-start.3
  202.8 4.0 %collective-permute-start.2 = (bf16[512,256]{1,0:T(8,128)(2,1)S(1)}, bf16[512,256]{1,0:T(8,128)(2,1)S(1)}, u32[]{:S(2)}, u32[]{:S(2)}) collective-permute-start(bf16[512,256]{1,0:T(8,128)(2,1)S(1)} %convolution_convert_fusion), channel_id=1, source_target_pairs={{0,4},{4,8},{8,12},{12,16},{16,20},{20,24},{24,28},{28,32},{32,36}... | collective-permute-start | bytes 786440 | tf_op jit(solution)/shard_map/ppermute | solution.py:44
  207.0 5.8 %all-to-all-done.6 = bf16[32,4,256]{2,1,0:T(4,128)(2,1)S(1)} async-done(((bf16[32,4,256]{2,1,0:T(4,128)(2,1)}), bf16[32,4,256]{2,1,0:T(4,128)(2,1)S(1)}, u32[]{:S(2)}, u32[]{:S(2)}) %all-to-all-start.6) | async-done | bytes 65568 | tf_op jit(solution)/shard_map/all_to_all | solution.py:21
  212.7 17.0 %all_to_all.60 = f32[32,4,256]{2,1,0:T(4,128)S(1)} all-to-all(f32[32,4,256]{2,1,0:T(4,128)S(1)} %reduce_sum.38), channel_id=1, replica_groups=mesh['rows_0'=8,'rows_1'=4,'rows_2'=4,'feat'=4] {'rows_0','rows_1'}, dimensions={0} | all-to-all | bytes 262144 | tf_op jit(solution)/shard_map/all_to_all | solution.py:67
  230.5 5.4 %all-to-all-start.7 = ((bf16[4,32,4,256]{3,2,1,0:T(4,128)(2,1)}), bf16[4,32,4,256]{3,2,1,0:T(4,128)(2,1)S(1)}, u32[]{:S(2)}, u32[]{:S(2)}) async-start(bf16[4,32,4,256]{3,2,1,0:T(4,128)(2,1)} %broadcast_in_dim.38), calls=%async_computation.7 | async-start | bytes 524288 | tf_op jit(solution)/shard_map/all_to_all | solution.py:21
  236.0 2.0 gather_fusion.1
  238.1 3.4 %all-to-all-done.7 = bf16[4,32,4,256]{3,2,1,0:T(4,128)(2,1)S(1)} async-done(((bf16[4,32,4,256]{3,2,1,0:T(4,128)(2,1)}), bf16[4,32,4,256]{3,2,1,0:T(4,128)(2,1)S(1)}, u32[]{:S(2)}, u32[]{:S(2)}) %all-to-all-start.7) | async-done | bytes 262176 | tf_op jit(solution)/shard_map/all_to_all | solution.py:21
  242.1 5.2 %all-to-all-start.10 = ((f32[32,4,256]{2,1,0:T(4,128)}), f32[32,4,256]{2,1,0:T(4,128)S(1)}, u32[]{:S(2)}, u32[]{:S(2)}) async-start(f32[32,4,256]{2,1,0:T(4,128)} %broadcast_in_dim.39), calls=%async_computation.10 | async-start | bytes 262144 | tf_op jit(solution)/shard_map/all_to_all | solution.py:21
  247.3 4.3 %convolution_bitcast_fusion = f32[32,128,256]{1,2,0:T(8,128)} fusion(bf16[32,128,256]{2,1,0:T(8,128)(2,1)} %gather_fusion.1, bf16[32,128,128]{2,1,0:T(8,128)(2,1)S(1)} %copy-done), kind=kOutput, calls=%fused_computation.2 | convolution fusion | flops 268435456 | bytes 7340032 | tf_op jit(solution)/shard_map/sij,sjf->sif/dot_general | solution.py:140
  251.6 5.5 %copy.66 = f32[32,128,256]{2,0,1:T(8,128)} copy(f32[32,128,256]{1,2,0:T(8,128)} %convolution_bitcast_fusion) | data formatting | bytes 8388608 | tf_op jit(solution)/shard_map/sij,sjf->sif/dot_general | solution.py:140
  257.1 1.3 all-to-all-done.10
  258.4 0.9 broadcast_in_dim.40
  259.2 3.5 %all-to-all-start.11 = ((f32[4,32,4,256]{3,2,1,0:T(4,128)}), f32[4,32,4,256]{3,2,1,0:T(4,128)S(1)}, u32[]{:S(2)}, u32[]{:S(2)}) async-start(f32[4,32,4,256]{3,2,1,0:T(4,128)} %broadcast_in_dim.40), calls=%async_computation.11 | async-start | bytes 1048576 | tf_op jit(solution)/shard_map/all_to_all | solution.py:21
  262.7 3.6 %fusion.21 = f32[4,128,256]{2,0,1:T(4,128)S(1)} fusion(f32[32,128,256]{2,0,1:T(8,128)} %copy.66, s32[32]{0:T(128)S(1)} %get-tuple-element.2), kind=kOutput, calls=%fused_computation.43 | convolution fusion | flops 50331776 | bytes 4718720 | tf_op jit(solution)/shard_map/rs,sif->rif/dot_general | solution.py:141
  267.4 1.1 fusion.1
  268.5 1.1 all-to-all-done.11
  (62 shorter events, 12.8 us)
Async XLA Ops:
  7.2 111.3 %copy-start = (bf16[32,128,128]{2,1,0:T(8,128)(2,1)S(1)}, bf16[32,128,128]{2,1,0:T(8,128)(2,1)}, u32[]{:S(2)}) copy-start(bf16[32,128,128]{2,1,0:T(8,128)(2,1)} %param.14) | copy-start | bytes 3145732
  7.2 35.2 %all-gather.3.cloned.1.call-start = ((), (), s32[]{:S(2)}) async-start(), calls=%async_computation.12 | async-start | bytes 1331200 | tf_op jit(solution)/shard_map/all_gather | solution.py:12
  8.0 36.2 %copy-start.1 = (bf16[512,512]{1,0:T(8,128)(2,1)S(1)}, bf16[512,512]{1,0:T(8,128)(2,1)}, u32[]{:S(2)}) copy-start(bf16[512,512]{1,0:T(8,128)(2,1)} %param.17) | copy-start | bytes 1572868
  44.6 5.5 %copy-start.3 = (s32[512]{0:T(512)S(1)}, s32[512]{0:T(512)}, u32[]{:S(2)}) copy-start(s32[512]{0:T(512)} %param.19) | copy-start | bytes 6148
  44.8 27.9 %copy-start.5 = (s32[32,3]{0,1:T(4,128)S(1)}, s32[32,3]{0,1:T(4,128)}, u32[]{:S(2)}) copy-start(s32[32,3]{0,1:T(4,128)} %param.13) | copy-start | bytes 1156
  45.0 45.5 %copy-start.4 = (s32[512]{0:T(512)S(1)}, s32[512]{0:T(512)}, u32[]{:S(2)}) copy-start(s32[512]{0:T(512)} %param.18) | copy-start | bytes 6148
  45.8 13.8 %all-to-all-start.2 = ((f32[4,32,4,256]{3,2,1,0:T(4,128)}), f32[4,32,4,256]{3,2,1,0:T(4,128)S(1)}, u32[]{:S(2)}, u32[]{:S(2)}) async-start(f32[4,32,4,256]{3,2,1,0:T(4,128)} %copy.62), calls=%async_computation.2 | async-start | bytes 1048576 | tf_op jit(solution)/shard_map/all_to_all | solution.py:60
  60.3 23.6 %all-to-all-start = ((bf16[32,4,256]{2,1,0:T(4,128)(2,1)}), bf16[32,4,256]{2,1,0:T(4,128)(2,1)S(1)}, u32[]{:S(2)}, u32[]{:S(2)}) async-start(bf16[32,4,256]{2,1,0:T(4,128)(2,1)} %broadcast_in_dim.33), calls=%async_computation | async-start | bytes 131072 | tf_op jit(solution)/shard_map/all_to_all | solution.py:21
  72.7 35.3 %collective-permute-start.1 = (bf16[512,256]{1,0:T(8,128)(2,1)S(1)}, bf16[512,256]{1,0:T(8,128)(2,1)S(1)}, u32[]{:S(2)}, u32[]{:S(2)}) collective-permute-start(bf16[512,256]{1,0:T(8,128)(2,1)S(1)} %convolution_convert_fusion.1), channel_id=1, source_target_pairs={{4,0},{8,4},{12,8},{16,12},{20,16},{24,20},{28,24},{32,28},{36,32}... | collective-permute-start | bytes 786440 | tf_op jit(solution)/shard_map/ppermute | solution.py:46
  74.0 34.0 %collective-permute-start = (bf16[512,256]{1,0:T(8,128)(2,1)S(1)}, bf16[512,256]{1,0:T(8,128)(2,1)}, u32[]{:S(2)}, u32[]{:S(2)}) collective-permute-start(bf16[512,256]{1,0:T(8,128)(2,1)S(1)} %convolution_convert_fusion.1), channel_id=1, source_target_pairs={{0,4},{4,8},{8,12},{12,16},{16,20},{20,24},{24,28},{28,32},{32,36}... | collective-permute-start | bytes 786440 | tf_op jit(solution)/shard_map/ppermute | solution.py:44
  83.8 17.9 %all-to-all-start.3 = ((f32[32,4,256]{2,1,0:T(4,128)}), f32[32,4,256]{2,1,0:T(4,128)S(1)}, u32[]{:S(2)}, u32[]{:S(2)}) async-start(f32[32,4,256]{2,1,0:T(4,128)} %reduce_sum.36), calls=%async_computation.3 | async-start | bytes 262144 | tf_op jit(solution)/shard_map/all_to_all | solution.py:67
  102.5 11.0 %all-to-all-start.1 = ((bf16[4,32,4,256]{3,2,1,0:T(4,128)(2,1)}), bf16[4,32,4,256]{3,2,1,0:T(4,128)(2,1)S(1)}, u32[]{:S(2)}, u32[]{:S(2)}) async-start(bf16[4,32,4,256]{3,2,1,0:T(4,128)(2,1)} %broadcast_in_dim.34), calls=%async_computation.1 | async-start | bytes 524288 | tf_op jit(solution)/shard_map/all_to_all | solution.py:21
  114.2 15.5 %all-to-all-start.4 = ((f32[32,4,256]{2,1,0:T(4,128)}), f32[32,4,256]{2,1,0:T(4,128)S(1)}, u32[]{:S(2)}, u32[]{:S(2)}) async-start(f32[32,4,256]{2,1,0:T(4,128)} %broadcast_in_dim.35), calls=%async_computation.4 | async-start | bytes 262144 | tf_op jit(solution)/shard_map/all_to_all | solution.py:21
  130.5 10.4 %all-to-all-start.5 = ((f32[4,32,4,256]{3,2,1,0:T(4,128)}), f32[4,32,4,256]{3,2,1,0:T(4,128)S(1)}, u32[]{:S(2)}, u32[]{:S(2)}) async-start(f32[4,32,4,256]{3,2,1,0:T(4,128)} %broadcast_in_dim.36), calls=%async_computation.5 | async-start | bytes 1048576 | tf_op jit(solution)/shard_map/all_to_all | solution.py:21
  134.0 37.3 %all-gather.5.cloned.1.call-start = ((), (), s32[]{:S(2)}) async-start(), calls=%async_computation.13 | async-start | bytes 1331200 | tf_op jit(solution)/shard_map/all_gather | solution.py:12
  137.7 0.7 copy-start.7
  173.7 5.3 %copy-start.2 = (bf16[2,1024,256]{2,1,0:T(8,128)(2,1)S(1)}, bf16[2,1024,256]{2,1,0:T(8,128)(2,1)}, u32[]{:S(2)}) copy-start(bf16[2,1024,256]{2,1,0:T(8,128)(2,1)} %param.12) | copy-start | bytes 3145732
  174.7 13.8 %all-to-all-start.8 = ((f32[4,32,4,256]{3,2,1,0:T(4,128)}), f32[4,32,4,256]{3,2,1,0:T(4,128)S(1)}, u32[]{:S(2)}, u32[]{:S(2)}) async-start(f32[4,32,4,256]{3,2,1,0:T(4,128)} %copy.70), calls=%async_computation.8 | async-start | bytes 1048576 | tf_op jit(solution)/shard_map/all_to_all | solution.py:60
  189.1 23.6 %all-to-all-start.6 = ((bf16[32,4,256]{2,1,0:T(4,128)(2,1)}), bf16[32,4,256]{2,1,0:T(4,128)(2,1)S(1)}, u32[]{:S(2)}, u32[]{:S(2)}) async-start(bf16[32,4,256]{2,1,0:T(4,128)(2,1)} %broadcast_in_dim.37), calls=%async_computation.6 | async-start | bytes 131072 | tf_op jit(solution)/shard_map/all_to_all | solution.py:21
  201.5 34.4 %collective-permute-start.3 = (bf16[512,256]{1,0:T(8,128)(2,1)S(1)}, bf16[512,256]{1,0:T(8,128)(2,1)S(1)}, u32[]{:S(2)}, u32[]{:S(2)}) collective-permute-start(bf16[512,256]{1,0:T(8,128)(2,1)S(1)} %convolution_convert_fusion), channel_id=1, source_target_pairs={{4,0},{8,4},{12,8},{16,12},{20,16},{24,20},{28,24},{32,28},{36,32}... | collective-permute-start | bytes 786440 | tf_op jit(solution)/shard_map/ppermute | solution.py:46
  202.8 33.1 %collective-permute-start.2 = (bf16[512,256]{1,0:T(8,128)(2,1)S(1)}, bf16[512,256]{1,0:T(8,128)(2,1)S(1)}, u32[]{:S(2)}, u32[]{:S(2)}) collective-permute-start(bf16[512,256]{1,0:T(8,128)(2,1)S(1)} %convolution_convert_fusion), channel_id=1, source_target_pairs={{0,4},{4,8},{8,12},{12,16},{16,20},{20,24},{24,28},{28,32},{32,36}... | collective-permute-start | bytes 786440 | tf_op jit(solution)/shard_map/ppermute | solution.py:44
  230.5 11.0 %all-to-all-start.7 = ((bf16[4,32,4,256]{3,2,1,0:T(4,128)(2,1)}), bf16[4,32,4,256]{3,2,1,0:T(4,128)(2,1)S(1)}, u32[]{:S(2)}, u32[]{:S(2)}) async-start(bf16[4,32,4,256]{3,2,1,0:T(4,128)(2,1)} %broadcast_in_dim.38), calls=%async_computation.7 | async-start | bytes 524288 | tf_op jit(solution)/shard_map/all_to_all | solution.py:21
  242.1 16.2 %all-to-all-start.10 = ((f32[32,4,256]{2,1,0:T(4,128)}), f32[32,4,256]{2,1,0:T(4,128)S(1)}, u32[]{:S(2)}, u32[]{:S(2)}) async-start(f32[32,4,256]{2,1,0:T(4,128)} %broadcast_in_dim.39), calls=%async_computation.10 | async-start | bytes 262144 | tf_op jit(solution)/shard_map/all_to_all | solution.py:21
  259.2 10.4 %all-to-all-start.11 = ((f32[4,32,4,256]{3,2,1,0:T(4,128)}), f32[4,32,4,256]{3,2,1,0:T(4,128)S(1)}, u32[]{:S(2)}, u32[]{:S(2)}) async-start(f32[4,32,4,256]{3,2,1,0:T(4,128)} %broadcast_in_dim.40), calls=%async_computation.11 | async-start | bytes 1048576 | tf_op jit(solution)/shard_map/all_to_all | solution.py:21
  266.3 1.0 copy-start.6
Sparse Core Ops, SparseCore 0:
  10.7 31.7 all-gather.2
  142.1 29.1 all-gather.4
where the time goes:
time: 283 us; the launch traced here: 277 us
  waiting for transfers between devices  111 us (39%)
  starting transfers between devices  78.5 us (28%)
  local copies, waits for them, and re-layouts  25.6 us (9%)
  matrix products  24.8 us (9%)
  blocking collectives  17 us (6%)
  between operations  14.4 us (5%)
  other arithmetic  6.13 us (2%)
    all_gather x2, waiting for transfers between devices, side_by_side(): lax.all_gather(both, axis, axis=dim, tiled=True)  61.8 us
    all_to_all x8, starting transfers between devices, sent_to_all(): return lax.all_to_all(copies, axis, split_axis=0, concat_axis=0, tiled=True)  52 us
    all_to_all x8, waiting for transfers between devices, sent_to_all(): return lax.all_to_all(copies, axis, split_axis=0, concat_axis=0, tiled=True)  20.9 us
    all_to_all x1, blocking collectives, sum_in_two_steps(): return jnp.sum(lax.all_to_all(own, far, 0, 0, tiled=True), axis=0)  17 us
    all_to_all x2, waiting for transfers between devices, sent_and_summed(): parts = lax.all_to_all(in_blocks(shard, dim, size), axis, 0, 0, tiled=True)  16.9 us
    all_to_all x1, waiting for transfers between devices, sum_in_two_steps(): return jnp.sum(lax.all_to_all(own, far, 0, 0, tiled=True), axis=0)  11.2 us
    dot_general x2, local copies, waits for them, and re-layouts, body(): jnp.einsum('sij,sjf->sif', tile_vals, picked, preferred_element_type=jnp....  11 us
    ppermute x2, starting transfers between devices, extended(): lax.ppermute(tail, axis, [(i, (i + 1) % count) for i in range(ends)])  8.7 us
  transfers between devices with their start and end apart: 17, of which 13 were waited for; matrix products, arithmetic and copies ran while one was open for 14% of the time, Pallas kernels for 0%

commit v1 on v0

v1 whole, which is shorter than its diff:
```python
import functools

import jax
import jax.numpy as jnp
from jax import lax
from jax.experimental import pallas as pl
from jax.experimental.pallas import tpu as pltpu
from jax.sharding import Mesh
from jax.sharding import PartitionSpec as P

MESH = pl.DeviceIdType.MESH
F32, BF16 = jnp.float32, jnp.bfloat16
NZ, NY, NX, NL, NC = 4, 4, 8, 2, 2
ROWS = ("z", "yh", "x")
FEAT = ("yl", "core")
TILE = 128
CHUNKS = 4


def dot(a, b):
    return jnp.dot(a, b, preferred_element_type=F32)


def down_rows(line):
    return jnp.broadcast_to(line, (TILE, line.shape[-1])).T


def kernel(
    place,
    deg,
    hdeg,
    reach,
    x_hbm,
    h_hbm,
    w_hbm,
    t_hbm,
    c_hbm,
    r_hbm,
    band_out,
    head_out,
    xin,
    hin,
    wts,
    tiles,
    cols,
    rws,
    dense,
    gath,
    win,
    acc,
    part,
    part_b,
    zin,
    ysrc,
    yin,
    xsrc,
    xin_h,
    feat_h,
    h4,
    head,
    hscale,
    bscale,
    cell,
    lsem,
    ssem,
    rsem,
):
    z, yh, x = (lax.axis_index(a) for a in ROWS)
    yl, core = (lax.axis_index(a) for a in FEAT)
    rank = (z * NY + yh) * NX + x
    me_f = yl * NC + core
    rows = xin.shape[0]
    step_rows = rows // CHUNKS
    tile_rows = rows // TILE
    has_left, has_right = rank > 0, rank < NZ * NY * NX - 1

    def at_rank(r):
        return {"z": r // (NY * NX), "yh": (r // NX) % NY, "x": r % NX}

    left = at_rank(jnp.maximum(rank - 1, 0))
    right = at_rank(jnp.minimum(rank + 1, NZ * NY * NX - 1))
    z_peers = [{"z": (z + k) % NZ} for k in range(1, NZ)]
    y_peers = [{"yh": (yh + k) % NY} for k in range(1, NY)]
    x_peers = [{"x": (x + k) % NX} for k in range(1, NX)]
    mate = {"core": 1 - core}
    across = {"yl": 1 - yl}
    f_peers = [mate, across, {"yl": 1 - yl, "core": 1 - core}]
    f_slots = [yl * NC + 1 - core, (1 - yl) * NC + core, (1 - yl) * NC + 1 - core]

    used = [0]
    started = []

    def remote(src, dst, device):
        i = used[0]
        used[0] += 1
        return pltpu.make_async_remote_copy(
            src_ref=src,
            dst_ref=dst,
            send_sem=ssem.at[i],
            recv_sem=rsem.at[i],
            device_id=device,
            device_id_type=MESH,
        )

    def push(src, dst, device):
        copy = remote(src, dst, device)
        copy.start()
        started.append(copy)
        return copy

    barrier = pltpu.get_barrier_semaphore()
    greet = z_peers + y_peers + x_peers + f_peers
    for peer in greet:
        pl.semaphore_signal(barrier, inc=1, device_id=peer, device_id_type=MESH)

    @pl.when(has_left)
    def _():
        pl.semaphore_signal(barrier, inc=1, device_id=left, device_id_type=MESH)

    @pl.when(has_right)
    def _():
        pl.semaphore_signal(barrier, inc=1, device_id=right, device_id_type=MESH)

    loads = []
    for i, (src, dst) in enumerate(
        ((x_hbm, xin), (h_hbm, hin), (r_hbm, rws), (t_hbm, tiles), (w_hbm, wts), (c_hbm, cols))
    ):
        load = pltpu.make_async_copy(src, dst, lsem.at[i])
        load.start()
        loads.append(load)
    load_x, load_h, load_r, load_t, load_w, load_c = loads

    load_h.wait()
    h4[pl.ds(x, 1)] = hin[...][None]
    load_x.wait()
    gath[0, pl.ds(me_f, 1)] = xin[...].astype(BF16)[None]
    load_r.wait()

    def head_partial(step):
        part[...] = dot(rws[...], gath[step, me_f]).reshape(part.shape)
        part_b[step] = part[...].astype(BF16)

    head_partial(0)
    pl.semaphore_wait(
        barrier, len(greet) + has_left.astype(jnp.int32) + has_right.astype(jnp.int32)
    )

    def z_start(step):
        return [
            push(part_b.at[step, (z + k) % NZ], zin.at[step, k - 1], z_peers[k - 1])
            for k in range(1, NZ)
        ]

    def z_finish(step, copies):
        total = part[z]
        for k in range(1, NZ):
            copies[k - 1].wait_recv()
            total = total + zin[step, k - 1].astype(F32)
        ysrc[step] = total.reshape(NY, -1, total.shape[-1])
        return [
            push(ysrc.at[step, (yh + k) % NY], yin.at[step, k - 1], y_peers[k - 1])
            for k in range(1, NY)
        ]

    def y_finish(step, copies):
        total = ysrc[step, yh]
        for k in range(1, NY):
            copies[k - 1].wait_recv()
            total = total + yin[step, k - 1]
        acc_x[0] = total
        xsrc[step] = total.astype(BF16)
        return [
            push(xsrc.at[step], xin_h.at[step, k - 1], x_peers[k - 1]) for k in range(1, NX)
        ]

    acc_x = [None]

    def x_finish(step, copies):
        for copy in copies:
            copy.wait_recv()
        total = xsrc[step].astype(F32)
        for k in range(1, NX):
            total = total + xin_h[step, k - 1].astype(F32)
        return total

    def feat_start(i, value):
        feat_h[i, pl.ds(me_f, 1)] = value.astype(BF16)[None]
        return [push(feat_h.at[i, me_f], feat_h.at[i, me_f], peer) for peer in f_peers]

    def feat_finish(i, step, copies):
        for copy in copies:
            copy.wait_recv()
        width = feat_h.shape[-1]
        return sum(
            dot(feat_h[i, f], wts[step, f * width : (f + 1) * width, :]) for f in range(NL * NC)
        )

    def gather_start(step):
        own = push(gath.at[step, me_f], gath.at[step, me_f], mate)
        over = []
        for i in range(CHUNKS):
            part_of = gath.at[step, me_f, pl.ds(i * step_rows, step_rows)]
            over.append(push(part_of, part_of, across))
        return own, over

    def hand_on(step, over, i):
        over[i].wait_recv()
        came = gath.at[step, f_slots[1], pl.ds(i * step_rows, step_rows)]
        return push(came, came, mate)

    def mix(step, i):
        width = gath.shape[-1]
        at = slice(i * step_rows, (i + 1) * step_rows)
        mixed = sum(
            dot(gath[step, f, at, :], wts[step, f * width : (f + 1) * width, :])
            for f in range(NL * NC)
        ).astype(BF16)
        win[step, rows + i * step_rows : rows + (i + 1) * step_rows, :] = mixed
        src = win.at[step, pl.ds(rows + i * step_rows, step_rows)]
        to_right = remote(src, win.at[step, pl.ds(i * step_rows, step_rows)], right)
        to_left = remote(src, win.at[step, pl.ds(2 * rows + i * step_rows, step_rows)], left)

        @pl.when(has_right)
        def _():
            to_right.start()

        @pl.when(has_left)
        def _():
            to_left.start()

        return to_right, to_left

    def halo_finish(pairs):
        @pl.when(has_left)
        def _():
            for to_right, _unused in pairs:
                to_right.wait_recv()

        @pl.when(has_right)
        def _():
            for _unused, to_left in pairs:
                to_left.wait_recv()

    def halo_sent(pairs):
        @pl.when(has_right)
        def _():
            for to_right, _unused in pairs:
                to_right.wait_send()

        @pl.when(has_left)
        def _():
            for _unused, to_left in pairs:
                to_left.wait_send()

    def head_spread(step, value):
        head[step, z, yh] = value.astype(BF16)
        src = head.at[step, z, yh]
        along_y = [push(src, src, peer) for peer in y_peers]
        along_z = [push(src, src, peer) for peer in z_peers]
        return along_y, along_z

    def head_hand_on(step, along_y, along_z):
        for k in range(1, NY):
            along_y[k - 1].wait_recv()
            src = head.at[step, z, (yh + NY - k) % NY]
            along_z = along_z + [push(src, src, peer) for peer in z_peers]
        return along_z

    def head_finish(step, along_z):
        for copy in along_z:
            copy.wait_recv()
        return head[step].reshape(-1, head.shape[-1])

    heads_x = [push(h4.at[x], h4.at[x], peer) for peer in x_peers]
    own0, over0 = gather_start(0)
    z0 = z_start(0)

    load_t.wait()
    n_tiles = tiles.shape[0]
    for s in range(n_tiles):
        cell[s] = place[s, 0] * (3 * tile_rows) + (place[s, 2] + 1) * tile_rows + place[s, 1]

    def build(first, last):
        def one(i, carry):
            total = jnp.zeros((TILE, TILE), BF16)
            for s in range(n_tiles):
                total = total + jnp.where(cell[s] == i, tiles[s], jnp.zeros((TILE, TILE), BF16))
            r, w = i // (3 * tile_rows), i % (3 * tile_rows)
            dense[
                pl.ds(pl.multiple_of(r * TILE, TILE), TILE),
                pl.ds(pl.multiple_of(w * TILE, TILE), TILE),
            ] = total
            return carry

        lax.fori_loop(first, last, one, 0)

    n_cells = tile_rows * 3 * tile_rows
    quarter = n_cells // 4
    build(0, quarter)

    @pl.when(jnp.logical_not(has_left))
    def _():
        for step in range(2):
            win[step, :rows] = jnp.zeros((rows, win.shape[-1]), BF16)

    @pl.when(jnp.logical_not(has_right))
    def _():
        for step in range(2):
            win[step, 2 * rows :] = jnp.zeros((rows, win.shape[-1]), BF16)

    for copy in heads_x:
        copy.wait_recv()
    load_w.wait()
    h_rows = jnp.concatenate([h4[k] for k in range(NX)], axis=0)
    feat_a = feat_start(0, h_rows)
    hand0 = [hand_on(0, over0, 0)]
    y0 = z_finish(0, z0)
    hand0.append(hand_on(0, over0, 1))
    along_y, along_z = head_spread(0, feat_finish(0, 0, feat_a))
    build(quarter, 2 * quarter)
    hand0.append(hand_on(0, over0, 2))
    own0.wait_recv()
    hand0[0].wait_recv()
    halo0 = [mix(0, 0)]
    build(2 * quarter, 3 * quarter)
    hand0.append(hand_on(0, over0, 3))
    hand0[1].wait_recv()
    halo0.append(mix(0, 1))
    hand0[2].wait_recv()
    halo0.append(mix(0, 2))
    along_z = head_hand_on(0, along_y, along_z)
    hand0[3].wait_recv()
    halo0.append(mix(0, 3))
    x0 = y_finish(0, y0)
    build(3 * quarter, n_cells)

    load_c.wait()
    for i in range(tile_rows):
        at = slice(i * TILE, (i + 1) * TILE)
        limit = down_rows(reach[i : i + 1, :])
        bscale[at, :] = lax.rsqrt(down_rows(deg[i : i + 1, :].astype(F32)))
        for j in range(cols.shape[1] // TILE):
            lane = lax.broadcasted_iota(jnp.int32, (TILE, TILE), 1) + j * TILE
            block = cols[at, j * TILE : (j + 1) * TILE]
            cols[at, j * TILE : (j + 1) * TILE] = jnp.where(
                lane < limit, block.astype(F32), 0.0
            ).astype(BF16)
    hscale[...] = lax.rsqrt(down_rows(hdeg[pl.ds(z, 1), :].astype(F32)))
    per_head = hscale.shape[0] // NY
    h_scale = hscale[pl.ds(pl.multiple_of(yh * per_head, per_head), per_head), :]
    h_scale = jnp.concatenate([h_scale, h_scale], axis=1)

    def own_band(step):
        acc[...] = dot(dense[:, rows : 2 * rows], win[step, rows : 2 * rows, :])

    def halo_band(step):
        acc[...] += dot(dense[:, :rows], win[step, :rows, :]) + dot(
            dense[:, 2 * rows :], win[step, 2 * rows :, :]
        )

    def state(step, along):
        whole = head_finish(step, along)
        scale = jnp.concatenate([bscale[...], bscale[...]], axis=1)
        return jnp.maximum((acc[...] + dot(cols[...], whole)) * scale, 0.0)

    own_band(0)
    halo_finish(halo0)
    halo_band(0)
    gath[1, pl.ds(me_f, 1)] = state(0, along_z).astype(BF16)[None]
    own1, over1 = gather_start(1)
    head_partial(1)
    z1 = z_start(1)

    feat_b = feat_start(1, x_finish(0, x0))
    h1 = jnp.maximum(feat_finish(1, 0, feat_b) * h_scale, 0.0)
    feat_c = feat_start(2, h1)
    hand1 = [hand_on(1, over1, 0)]
    along_y, along_z = head_spread(1, feat_finish(2, 1, feat_c))
    hand1.append(hand_on(1, over1, 1))
    own1.wait_recv()
    hand1[0].wait_recv()
    halo1 = [mix(1, 0)]
    y1 = z_finish(1, z1)
    hand1.append(hand_on(1, over1, 2))
    hand1[1].wait_recv()
    halo1.append(mix(1, 1))
    hand1.append(hand_on(1, over1, 3))
    hand1[2].wait_recv()
    halo1.append(mix(1, 2))
    along_z = head_hand_on(1, along_y, along_z)
    hand1[3].wait_recv()
    halo1.append(mix(1, 3))
    x1 = y_finish(1, y1)
    own_band(1)
    halo_finish(halo1)
    halo_band(1)
    band_out[...] = state(1, along_z)
    feat_d = feat_start(3, x_finish(1, x1))
    h2 = jnp.maximum(feat_finish(3, 1, feat_d) * h_scale, 0.0)
    per = head_out.shape[0]
    mine = jnp.zeros(head_out.shape, F32)
    for k in range(NX):
        mine = mine + jnp.where(x == k, h2[k * per : (k + 1) * per, :], 0.0)
    head_out[...] = mine

    for copy in started:
        copy.wait_send()
    halo_sent(halo0)
    halo_sent(halo1)


N_COPIES = 256


def body(
    band_feats,
    head_feats,
    mix_weights,
    tile_place,
    tile_vals,
    arrow_cols,
    arrow_reach,
    arrow_rows,
    band_degree,
    head_degree,
):
    rows, width = band_feats.shape
    heads = arrow_rows.shape[0]
    per_y = heads // (NZ * NY)
    vmem = pl.BlockSpec(memory_space=pltpu.VMEM)
    smem = pl.BlockSpec(memory_space=pltpu.SMEM)
    hbm = pl.BlockSpec(memory_space=pl.ANY)
    return pl.pallas_call(
        kernel,
        out_shape=(
            jax.ShapeDtypeStruct((rows, width), F32),
            jax.ShapeDtypeStruct(head_feats.shape, F32),
        ),
        in_specs=[smem, vmem, vmem, vmem] + [hbm] * 6,
        out_specs=(vmem, vmem),
        scratch_shapes=[
            pltpu.VMEM((rows, width), F32),
            pltpu.VMEM(head_feats.shape, F32),
            pltpu.VMEM(mix_weights.shape, BF16),
            pltpu.VMEM(tile_vals.shape, BF16),
            pltpu.VMEM(arrow_cols.shape, BF16),
            pltpu.VMEM(arrow_rows.shape, BF16),
            pltpu.VMEM((rows, 3 * rows), BF16),
            pltpu.VMEM((2, NL * NC, rows, width), BF16),
            pltpu.VMEM((2, 3 * rows, width), BF16),
            pltpu.VMEM((rows, width), F32),
            pltpu.VMEM((NZ, heads // NZ, width), F32),
            pltpu.VMEM((2, NZ, heads // NZ, width), BF16),
            pltpu.VMEM((2, NZ - 1, heads // NZ, width), BF16),
            pltpu.VMEM((2, NY, per_y, width), F32),
            pltpu.VMEM((2, NY - 1, per_y, width), F32),
            pltpu.VMEM((2, per_y, width), BF16),
            pltpu.VMEM((2, NX - 1, per_y, width), BF16),
            pltpu.VMEM((4, NL * NC, per_y, width), BF16),
            pltpu.VMEM((NX, *head_feats.shape), F32),
            pltpu.VMEM((2, NZ, NY, per_y, width), BF16),
            pltpu.VMEM((heads // NZ, TILE), F32),
            pltpu.VMEM((rows, TILE), F32),
            pltpu.SMEM((tile_vals.shape[0],), jnp.int32),
            pltpu.SemaphoreType.DMA((6,)),
            pltpu.SemaphoreType.DMA((N_COPIES,)),
            pltpu.SemaphoreType.DMA((N_COPIES,)),
        ],
        compiler_params=pltpu.CompilerParams(collective_id=0, has_side_effects=True),
    )(
        tile_place,
        band_degree.reshape(-1, TILE),
        head_degree.reshape(-1, TILE),
        arrow_reach.reshape(-1, TILE),
        band_feats,
        head_feats,
        mix_weights,
        tile_vals,
        arrow_cols,
        arrow_rows,
    )


def solution(mesh):
    split = Mesh(
        mesh.devices.reshape(NZ, NY, NX, NL, NC), (*ROWS, *FEAT)
    )
    return jax.shard_map(
        body,
        mesh=split,
        in_specs=(
            P(ROWS, FEAT),
            P(ROWS, FEAT),
            P(None, None, FEAT),
            P(ROWS, None),
            P(ROWS, None, None),
            P(ROWS, None),
            P(ROWS),
            P(None, ROWS),
            P(ROWS),
            P(),
        ),
        out_specs=(P(ROWS, FEAT), P(ROWS, FEAT)),
        check_vma=False,
    )
```

time: 283 us -> 87.9 us (0.31); the launches traced: 277 us -> 86.8 us
  waiting for transfers between devices: 111 us -> 0 us
  Pallas kernels: 0 us -> 82.4 us
  starting transfers between devices: 78.5 us -> 0 us
  matrix products: 24.8 us -> 0 us
  local copies, waits for them, and re-layouts: 25.6 us -> 3.83 us
  blocking collectives: 17 us -> 0 us
  between operations: 14.4 us -> 0.66 us
  other arithmetic: 6.13 us -> 0 us
    pallas_call x0 -> x1, Pallas kernels: none -> 82.4 us  [body(): pl.pallas_call(kernel, out_shape=(jax.ShapeDtypeStruct((rows, width), F32...]
    all_to_all x11 -> x0, starting transfers between devices: 67.2 us -> none  [the longest x8 52 us: sent_to_all(): return lax.all_to_all(copies, axis, split_axis=0, concat_axis=0, tiled=True)]
    all_gather x2 -> x0, waiting for transfers between devices: 61.8 us -> none  [side_by_side(): lax.all_gather(both, axis, axis=dim, tiled=True)]
    all_to_all x11 -> x0, waiting for transfers between devices: 49 us -> none  [the longest x8 20.9 us: sent_to_all(): return lax.all_to_all(copies, axis, split_axis=0, concat_axis=0, tiled=True)]
    dot_general x12 -> x0, matrix products: 24.8 us -> none  [the longest x2 8.62 us: body(): jnp.einsum('sij,sjf->sif', tile_vals, picked, preferred_element_type=jnp....]
    all_to_all x1 -> x0, blocking collectives: 17 us -> none  [sum_in_two_steps(): return jnp.sum(lax.all_to_all(own, far, 0, 0, tiled=True), axis=0)]
    dot_general x6 -> x0, local copies, waits for them, and re-layouts: 11.6 us -> none  [the longest x2 11 us: body(): jnp.einsum('sij,sjf->sif', tile_vals, picked, preferred_element_type=jnp....]
    ppermute x4 -> x0, starting transfers between devices: 11.3 us -> none  [the longest x2 8.7 us: extended(): lax.ppermute(tail, axis, [(i, (i + 1) % count) for i in range(ends)])]
  transfers between devices with their start and end apart: 17 -> 0, of which waited for: 13 -> 0; matrix products, arithmetic and copies ran while one was open for 14% -> 0% of each run, Pallas kernels for 0% -> 0%
where the time goes in v1:
time: 87.9 us; the launch traced here: 86.8 us
  Pallas kernels  82.4 us (94%)
  local copies, waits for them, and re-layouts  3.83 us (4%)
    pallas_call x1, Pallas kernels, body(): pl.pallas_call(kernel, out_shape=(jax.ShapeDtypeStruct((rows, width), F32...  82.4 us
    unnamed x7, local copies, waits for them, and re-layouts  3.83 us

profile of v1, /device:TPU:1, one launch (start us, length us, event | category | flops | bytes accessed | tf_op | source)
XLA Modules:
  0.0 86.8 jit_solution(16798459554517669574)
XLA Ops:
  0.6 0.0 copy-start.1
  0.6 0.7 copy-done.1
  1.3 0.7 copy.12.place
  2.0 82.4 %shard_map.113 = (f32[512,256]{1,0:T(8,128)}, f32[4,256]{1,0:T(4,128)}) custom-call(s32[32,3]{1,0:T(8,128)} %copy.12.place, s32[4,128]{1,0:T(4,128)} %bitcast.3, s32[4,128]{1,0:T(4,128)} %bitcast.4, s32[4,128]{1,0:T(4,128)} %bitcast.5, f32[512,256]{1,0:T(8,128)} %x_hbm.1, f32[4,256]{1,0:T(4,128)} %h_hbm.1, bf16[2,1024,256]{2,1,0:T(8,128)(2,1)} %w_hbm.1, ...), custom_call_target="tpu_custom_call" | custom-call | tf_op jit(solution)/shard_map/pallas_call | solution.py:433
  84.4 0.0 copy-start
  84.4 1.9 %copy.15 = f32[512,256]{1,0:T(8,128)} copy(f32[512,256]{1,0:T(8,128)} %get-tuple-element.4) | data formatting | bytes 1048576
  86.2 0.0 copy-done
  86.2 0.6 copy.16
Async XLA Ops:
  0.6 0.7 copy-start.1
  84.4 1.9 %copy-start = (f32[4,256]{1,0:T(4,128)S(1)}, f32[4,256]{1,0:T(4,128)}, u32[]{:S(2)}) copy-start(f32[4,256]{1,0:T(4,128)} %get-tuple-element.5) | copy-start | bytes 12292

commit v2 on v1

v2 whole, which is shorter than its diff:
```python
import functools

import jax
import jax.numpy as jnp
from jax import lax
from jax.experimental import pallas as pl
from jax.experimental.pallas import tpu as pltpu
from jax.sharding import Mesh
from jax.sharding import PartitionSpec as P

MESH = pl.DeviceIdType.MESH
F32, BF16 = jnp.float32, jnp.bfloat16
NZ, NY, NX, NL, NC = 8, 4, 4, 2, 2
ROWS = ("z", "yh", "x")
FEAT = ("yl", "core")
TILE = 128
CHUNKS = 4


def dot(a, b):
    return jnp.dot(a, b, preferred_element_type=F32)


def down_rows(line):
    return jnp.broadcast_to(line, (TILE, line.shape[-1])).T


def kernel(
    place,
    deg,
    hdeg,
    reach,
    x_hbm,
    h_hbm,
    w_hbm,
    t_hbm,
    c_hbm,
    r_hbm,
    band_out,
    head_out,
    xin,
    wts,
    tiles,
    cols,
    rws,
    rws_p,
    dense,
    gath,
    win,
    acc,
    part,
    part_b,
    xrcv,
    zsrc,
    zrcv,
    ysrc,
    yrcv,
    feat_h,
    hf,
    h4,
    relay,
    head,
    hscale,
    bscale,
    lines,
    table,
    lsem,
    ssem,
    rsem,
):
    z, yh, x = (lax.axis_index(a) for a in ROWS)
    yl, core = (lax.axis_index(a) for a in FEAT)
    rank = (z * NY + yh) * NX + x
    me_f = yl * NC + core
    rows = xin.shape[0]
    step_rows = rows // CHUNKS
    tile_rows = rows // TILE
    has_left, has_right = rank > 0, rank < NZ * NY * NX - 1

    def at_rank(r):
        return {"z": r // (NY * NX), "yh": (r // NX) % NY, "x": r % NX}

    left = at_rank(jnp.maximum(rank - 1, 0))
    right = at_rank(jnp.minimum(rank + 1, NZ * NY * NX - 1))
    z_order, y_order, x_order = [4, 3, 5, 2, 6, 1, 7], [2, 1, 3], [2, 1, 3]
    z_peers = {k: {"z": (z + k) % NZ} for k in z_order}
    y_peers = {k: {"yh": (yh + k) % NY} for k in y_order}
    x_peers = {k: {"x": (x + k) % NX} for k in x_order}
    last_x = NX - 1
    below, above = rank >= NX, rank < NZ * NY * NX - NX
    first_col, last_col = x == 0, x == last_x
    relay_right = jnp.logical_and(last_col, has_right)
    relay_left = jnp.logical_and(first_col, has_left)
    serve_right = jnp.logical_and(first_col, above)
    serve_left = jnp.logical_and(last_col, below)
    up = at_rank(jnp.minimum(rank + NX, NZ * NY * NX - 1))
    down = at_rank(jnp.maximum(rank - NX, 0))
    at_first, at_last = {"x": 0 * x}, {"x": 0 * x + last_x}
    corner = jnp.logical_or(first_col, last_col)
    greet_up, greet_down = jnp.logical_and(corner, above), jnp.logical_and(corner, below)
    mate = {"core": 1 - core}
    across = {"yl": 1 - yl}
    f_peers = [across, {"yl": 1 - yl, "core": 1 - core}, mate]
    far_slot = (1 - yl) * NC + core

    used = [0]
    started = []

    def remote(src, dst, device):
        i = used[0]
        used[0] += 1
        return pltpu.make_async_remote_copy(
            src_ref=src,
            dst_ref=dst,
            send_sem=ssem.at[i],
            recv_sem=rsem.at[i],
            device_id=device,
            device_id_type=MESH,
        )

    def push(src, dst, device):
        copy = remote(src, dst, device)
        copy.start()
        started.append(copy)
        return copy

    barrier = pltpu.get_barrier_semaphore()
    greet = [*z_peers.values(), *y_peers.values(), *x_peers.values(), *f_peers]
    for peer in greet:
        pl.semaphore_signal(barrier, inc=1, device_id=peer, device_id_type=MESH)

    @pl.when(has_left)
    def _():
        pl.semaphore_signal(barrier, inc=1, device_id=left, device_id_type=MESH)

    @pl.when(has_right)
    def _():
        pl.semaphore_signal(barrier, inc=1, device_id=right, device_id_type=MESH)

    @pl.when(greet_up)
    def _():
        pl.semaphore_signal(barrier, inc=1, device_id=up, device_id_type=MESH)

    @pl.when(greet_down)
    def _():
        pl.semaphore_signal(barrier, inc=1, device_id=down, device_id_type=MESH)

    def load(i, src, dst):
        copy = pltpu.make_async_copy(src, dst, lsem.at[i])
        copy.start()
        return copy

    load_x = load(0, x_hbm, xin)
    load_h = load(1, h_hbm, hf.at[me_f])
    load_r = load(2, r_hbm, rws)
    load_x.wait()
    load_w0 = load(3, w_hbm.at[0], wts.at[0])
    load_t = load(4, t_hbm, tiles.at[pl.ds(0, t_hbm.shape[0])])
    load_c = load(5, c_hbm, cols)
    load_w1 = load(6, w_hbm.at[1], wts.at[1])
    gath[0, pl.ds(me_f, 1)] = xin[...].astype(BF16)[None]
    load_h.wait()
    others = [has_left, has_right, greet_up, greet_down]
    pl.semaphore_wait(
        barrier, len(greet) + sum(there.astype(jnp.int32) for there in others)
    )

    def head_partial(step, weights):
        part[...] = dot(weights[...], gath[step, me_f]).reshape(part.shape)
        part_b[step] = part[...].astype(BF16)
        return [
            push(part_b.at[step, (x + k) % NX], xrcv.at[step, k - 1], x_peers[k]) for k in x_order
        ]

    def x_finish(step, copies):
        total = part[x]
        for copy in copies:
            copy.wait_recv()
        for k in range(1, NX):
            total = total + xrcv[step, k - 1].astype(F32)
        zsrc[step] = total.reshape(NZ, -1, total.shape[-1]).astype(BF16)
        return [
            push(zsrc.at[step, (z + k) % NZ], zrcv.at[step, k - 1], z_peers[k]) for k in z_order
        ]

    def z_finish(step, copies):
        for copy in copies:
            copy.wait_recv()
        total = zsrc[step, z].astype(F32)
        for k in range(1, NZ):
            total = total + zrcv[step, k - 1].astype(F32)
        ysrc[step] = total
        return [push(ysrc.at[step], yrcv.at[step, k - 1], y_peers[k]) for k in y_order]

    def y_finish(step, copies):
        for copy in copies:
            copy.wait_recv()
        total = ysrc[step]
        for k in range(1, NY):
            total = total + yrcv[step, k - 1]
        return total

    def feat_start(i, value):
        feat_h[i, pl.ds(me_f, 1)] = value.astype(BF16)[None]
        return [push(feat_h.at[i, me_f], feat_h.at[i, me_f], peer) for peer in f_peers]

    def feat_finish(i, step, copies):
        for copy in copies:
            copy.wait_recv()
        width = feat_h.shape[-1]
        return sum(
            dot(feat_h[i, f], wts[step, f * width : (f + 1) * width, :]) for f in range(NL * NC)
        )

    def over_send(step, i):
        part_of = gath.at[step, me_f, pl.ds(i * step_rows, step_rows)]
        return push(part_of, part_of, across)

    def gather_start(step, ahead):
        over = [over_send(step, i) for i in range(ahead)]
        own = push(gath.at[step, me_f], gath.at[step, me_f], mate)
        return own, over

    def hand_on(step, over, i):
        over[i].wait_recv()
        came = gath.at[step, far_slot, pl.ds(i * step_rows, step_rows)]
        return push(came, came, mate)

    def mix(step, i):
        width = gath.shape[-1]
        at = slice(i * step_rows, (i + 1) * step_rows)
        mixed = sum(
            dot(gath[step, f, at, :], wts[step, f * width : (f + 1) * width, :])
            for f in range(NL * NC)
        ).astype(BF16)
        win[step, rows + i * step_rows : rows + (i + 1) * step_rows, :] = mixed
        src = win.at[step, pl.ds(rows + i * step_rows, step_rows)]
        to_left_part = win.at[step, pl.ds(i * step_rows, step_rows)]
        to_right_part = win.at[step, pl.ds(2 * rows + i * step_rows, step_rows)]
        to_right = remote(src, to_left_part, right)
        to_left = remote(src, to_right_part, left)
        if i % 2:

            @pl.when(has_right)
            def _():
                to_right.start()

            @pl.when(has_left)
            def _():
                to_left.start()

            return to_right, to_left, None

        spare = relay.at[step, i // 2]
        by_first, by_last = remote(src, spare, at_first), remote(src, spare, at_last)
        used[0] -= 4
        pass_right = remote(spare, to_left_part, up)
        pass_left = remote(spare, to_right_part, down)
        used[0] += 2

        @pl.when(relay_right)
        def _():
            by_first.start()

        @pl.when(jnp.logical_and(has_right, jnp.logical_not(last_col)))
        def _():
            to_right.start()

        @pl.when(relay_left)
        def _():
            by_last.start()

        @pl.when(jnp.logical_and(has_left, jnp.logical_not(first_col)))
        def _():
            to_left.start()

        return to_right, to_left, (by_first, by_last, pass_right, pass_left)

    def relay_on(copies):
        by_first, by_last, pass_right, pass_left = copies[2]

        @pl.when(serve_right)
        def _():
            by_first.wait_recv()
            pass_right.start()

        @pl.when(serve_left)
        def _():
            by_last.wait_recv()
            pass_left.start()

    def halo_finish(halos):
        @pl.when(has_left)
        def _():
            for copies in halos:
                copies[0].wait_recv()

        @pl.when(has_right)
        def _():
            for copies in halos:
                copies[1].wait_recv()

    def halo_sent(halos):
        for copies in halos:
            if copies[2] is None:

                @pl.when(has_right)
                def _():
                    copies[0].wait_send()

                @pl.when(has_left)
                def _():
                    copies[1].wait_send()

                continue
            by_first, by_last, pass_right, pass_left = copies[2]

            @pl.when(relay_right)
            def _():
                by_first.wait_send()

            @pl.when(relay_left)
            def _():
                by_last.wait_send()

            @pl.when(serve_right)
            def _():
                pass_right.wait_send()

            @pl.when(serve_left)
            def _():
                pass_left.wait_send()

            @pl.when(jnp.logical_and(has_right, jnp.logical_not(last_col)))
            def _():
                copies[0].wait_send()

            @pl.when(jnp.logical_and(has_left, jnp.logical_not(first_col)))
            def _():
                copies[1].wait_send()

    piece = head.shape[-2]

    def spread(step, src, peers):
        def to_z(piece_ref):
            return [push(piece_ref, piece_ref, z_peers[k]) for k in z_order]

        return {k: push(src, src, peer) for k, peer in peers.items()}, to_z(src)

    def spread_y(value):
        head[0, z, yh] = value.astype(BF16)
        return spread(0, head.at[0, z, yh], y_peers)

    def hand_y(along_y, along_z):
        for k in (1, 3, 2):
            along_y[k].wait_recv()
            src = head.at[0, z, (yh + NY - k) % NY]
            along_z = along_z + [push(src, src, z_peers[q]) for q in z_order]
        return along_z

    def spread_x(value):
        head[1, z, x] = value.astype(BF16)
        return spread(1, head.at[1, z, x], x_peers)

    def hand_x(along_x, along_z):
        for k in (1, 3, 2):
            along_x[k].wait_recv()
            src = head.at[1, z, (x + NX - k) % NX]
            along_z = along_z + [push(src, src, z_peers[q]) for q in z_order]
        return along_z

    def head_finish(step, along_z):
        for copy in along_z:
            copy.wait_recv()
        if step:
            return jnp.concatenate([head[1, :, k].reshape(-1, head.shape[-1]) for k in range(NX)])
        return head[0].reshape(-1, head.shape[-1])

    n_tiles = place.shape[1]
    n_cols = 3 * tile_rows

    def tables():
        tile_row, tile_col, offset = (place[i : i + 1, :] for i in range(3))
        lines[...] = jnp.full(lines.shape, -1, jnp.int32)
        lines[0:1, :n_tiles] = tile_row * n_cols + (offset + 1) * tile_rows + tile_col
        line = lines[0:1, :]
        down = down_rows(line)[:n_tiles]
        slot = lax.broadcasted_iota(jnp.int32, down.shape, 0)
        lane = lax.broadcasted_iota(jnp.int32, down.shape, 1)
        later = jnp.where(jnp.logical_and(down == line, slot > lane), slot, n_tiles)
        first = jnp.where(down == lane, slot, n_tiles)
        lines[0:1, :] = jnp.min(later, axis=0, keepdims=True)
        lines[1:2, :] = jnp.min(first, axis=0, keepdims=True)
        copy = pltpu.make_async_copy(lines, table, lsem.at[7])
        copy.start()
        tiles[n_tiles] = jnp.zeros((TILE, TILE), BF16)
        return copy

    def build():
        for s in reversed(range(n_tiles - 1)):
            tiles[s] = tiles[s] + tiles[table[0, s]]
        for c in range(tile_rows * n_cols):
            r, w = c // n_cols, c % n_cols
            dense[r * TILE : (r + 1) * TILE, w * TILE : (w + 1) * TILE] = tiles[table[1, c]]

    def edges():
        @pl.when(jnp.logical_not(has_left))
        def _():
            for step in range(2):
                win[step, :rows] = jnp.zeros((rows, win.shape[-1]), BF16)

        @pl.when(jnp.logical_not(has_right))
        def _():
            for step in range(2):
                win[step, 2 * rows :] = jnp.zeros((rows, win.shape[-1]), BF16)

    def mask_cols(i):
        at = slice(i * TILE, (i + 1) * TILE)
        limit = down_rows(reach[i : i + 1, :])
        bscale[at, :] = lax.rsqrt(down_rows(deg[i : i + 1, :].astype(F32)))
        for j in range(cols.shape[1] // TILE):
            lane = lax.broadcasted_iota(jnp.int32, (TILE, TILE), 1) + j * TILE
            block = cols[at, j * TILE : (j + 1) * TILE]
            cols[at, j * TILE : (j + 1) * TILE] = jnp.where(
                lane < limit, block.astype(F32), 0.0
            ).astype(BF16)

    def permute_rows():
        per = head_out.shape[0]
        for g in range(NX):
            shape = (part.shape[1], rws.shape[0])
            to = lax.broadcasted_iota(jnp.int32, shape, 0)
            come = lax.broadcasted_iota(jnp.int32, shape, 1)
            source = (to // per) * (NX * per) + g * per + to % per
            pick = jnp.where(come == source, 1.0, 0.0).astype(BF16)
            rws_p[g * shape[0] : (g + 1) * shape[0], :] = dot(pick, rws[...]).astype(BF16)

    def own_band(step):
        acc[...] = dot(dense[:, rows : 2 * rows], win[step, rows : 2 * rows, :])

    def halo_band(step):
        acc[...] += dot(dense[:, :rows], win[step, :rows, :]) + dot(
            dense[:, 2 * rows :], win[step, 2 * rows :, :]
        )

    def state(step, along):
        whole = head_finish(step, along)
        scale = jnp.concatenate([bscale[...], bscale[...]], axis=1)
        return jnp.maximum((acc[...] + dot(cols[...], whole)) * scale, 0.0)

    heads_f = [push(hf.at[me_f], hf.at[me_f], peer) for peer in f_peers]
    own0, over0 = gather_start(0, CHUNKS)
    load_r.wait()
    x0 = head_partial(0, rws)
    tabled = tables()
    for copy in heads_f:
        copy.wait_recv()
    load_w0.wait()
    width = hf.shape[-1]
    h4[x] = sum(
        dot(hf[f].astype(BF16), wts[0, f * width : (f + 1) * width, :]) for f in range(NL * NC)
    )
    heads_x = [push(h4.at[x], h4.at[x], x_peers[k]) for k in x_order]
    load_t.wait()
    tabled.wait()
    build()
    hand0 = [hand_on(0, over0, 0)]
    for copy in heads_x:
        copy.wait_recv()
    along_y, along_z = spread_y(jnp.concatenate([h4[k] for k in range(NX)], axis=0))
    hand0.append(hand_on(0, over0, 1))
    own0.wait_recv()
    hand0[0].wait_recv()
    halo0 = [mix(0, 0)]
    z0 = x_finish(0, x0)
    hand0.append(hand_on(0, over0, 2))
    hand0[1].wait_recv()
    halo0.append(mix(0, 1))
    hand0.append(hand_on(0, over0, 3))
    hand0[2].wait_recv()
    relay_on(halo0[0])
    halo0.append(mix(0, 2))
    hand0[3].wait_recv()
    halo0.append(mix(0, 3))
    own_band(0)
    edges()
    load_c.wait()
    for i in range(tile_rows):
        mask_cols(i)
    y0 = z_finish(0, z0)
    along_z = hand_y(along_y, along_z)
    relay_on(halo0[2])
    permute_rows()
    hscale[...] = lax.rsqrt(down_rows(hdeg[pl.ds(x, 1), :].astype(F32)))
    h_scale = hscale[pl.ds(pl.multiple_of(z * piece, piece), piece), :]
    h_scale = jnp.concatenate([h_scale, h_scale], axis=1)
    halo_finish(halo0)
    halo_band(0)
    feat_b = feat_start(0, y_finish(0, y0))
    gath[1, pl.ds(me_f, 1)] = state(0, along_z).astype(BF16)[None]
    own1, over1 = gather_start(1, 2)
    x1 = head_partial(1, rws_p)
    h1 = jnp.maximum(feat_finish(0, 0, feat_b) * h_scale, 0.0)
    feat_c = feat_start(1, h1)
    over1 += [over_send(1, 2), over_send(1, 3)]
    hand1 = [hand_on(1, over1, 0)]
    load_w1.wait()
    hand1.append(hand_on(1, over1, 1))
    own1.wait_recv()
    hand1[0].wait_recv()
    halo1 = [mix(1, 0)]
    along_x, along_z = spread_x(feat_finish(1, 1, feat_c))
    z1 = x_finish(1, x1)
    hand1.append(hand_on(1, over1, 2))
    hand1[1].wait_recv()
    halo1.append(mix(1, 1))
    hand1.append(hand_on(1, over1, 3))
    hand1[2].wait_recv()
    halo1.append(mix(1, 2))
    hand1[3].wait_recv()
    halo1.append(mix(1, 3))
    relay_on(halo1[0])
    along_z = hand_x(along_x, along_z)
    y1 = z_finish(1, z1)
    own_band(1)
    relay_on(halo1[2])
    feat_d = feat_start(2, y_finish(1, y1))
    halo_finish(halo1)
    halo_band(1)
    band_out[...] = state(1, along_z)
    sums = feat_finish(2, 1, feat_d)
    per = head_out.shape[0]
    near_z = hscale.shape[0] // (per * NX * NY)
    hscale[...] = lax.rsqrt(down_rows(hdeg[pl.ds(z // near_z, 1), :].astype(F32)))
    at = pl.multiple_of((z % near_z) * NY * NX * per + yh * NX * per, NX * per)
    near = hscale[pl.ds(at, NX * per), :]
    near = jnp.concatenate([near, near], axis=1)
    mine, own_scale = jnp.zeros(head_out.shape, F32), jnp.zeros(head_out.shape, F32)
    for k in range(NY):
        mine = mine + jnp.where(yh == k, sums[k * per : (k + 1) * per, :], 0.0)
    for k in range(NX):
        own_scale = own_scale + jnp.where(x == k, near[k * per : (k + 1) * per, :], 0.0)
    head_out[...] = jnp.maximum(mine * own_scale, 0.0)

    for copy in started:
        copy.wait_send()
    halo_sent(halo0)
    halo_sent(halo1)


N_COPIES = 240


def body(
    band_feats,
    head_feats,
    mix_weights,
    tile_place,
    tile_vals,
    arrow_cols,
    arrow_reach,
    arrow_rows,
    band_degree,
    head_degree,
):
    rows, width = band_feats.shape
    heads = arrow_rows.shape[0]
    piece = heads // (NZ * NX)
    vmem = pl.BlockSpec(memory_space=pltpu.VMEM)
    hbm = pl.BlockSpec(memory_space=pl.ANY)
    return pl.pallas_call(
        kernel,
        out_shape=(
            jax.ShapeDtypeStruct((rows, width), F32),
            jax.ShapeDtypeStruct(head_feats.shape, F32),
        ),
        in_specs=[vmem] * 4 + [hbm] * 6,
        out_specs=(vmem, vmem),
        scratch_shapes=[
            pltpu.VMEM((rows, width), F32),
            pltpu.VMEM(mix_weights.shape, BF16),
            pltpu.VMEM((tile_vals.shape[0] + 1, TILE, TILE), BF16),
            pltpu.VMEM(arrow_cols.shape, BF16),
            pltpu.VMEM(arrow_rows.shape, BF16),
            pltpu.VMEM(arrow_rows.shape, BF16),
            pltpu.VMEM((rows, 3 * rows), BF16),
            pltpu.VMEM((2, NL * NC, rows, width), BF16),
            pltpu.VMEM((2, 3 * rows, width), BF16),
            pltpu.VMEM((rows, width), F32),
            pltpu.VMEM((NX, heads // NX, width), F32),
            pltpu.VMEM((2, NX, heads // NX, width), BF16),
            pltpu.VMEM((2, NX - 1, heads // NX, width), BF16),
            pltpu.VMEM((2, NZ, piece, width), BF16),
            pltpu.VMEM((2, NZ - 1, piece, width), BF16),
            pltpu.VMEM((2, piece, width), F32),
            pltpu.VMEM((2, NY - 1, piece, width), F32),
            pltpu.VMEM((3, NL * NC, piece, width), BF16),
            pltpu.VMEM((NL * NC, *head_feats.shape), F32),
            pltpu.VMEM((NX, *head_feats.shape), F32),
            pltpu.VMEM((2, 2, rows // CHUNKS, width), BF16),
            pltpu.VMEM((2, NZ, NX, piece, width), BF16),
            pltpu.VMEM((heads // NX, TILE), F32),
            pltpu.VMEM((rows, TILE), F32),
            pltpu.VMEM((8, TILE), jnp.int32),
            pltpu.SMEM((8, TILE), jnp.int32),
            pltpu.SemaphoreType.DMA((8,)),
            pltpu.SemaphoreType.DMA((N_COPIES,)),
            pltpu.SemaphoreType.DMA((N_COPIES,)),
        ],
        compiler_params=pltpu.CompilerParams(collective_id=0, has_side_effects=True),
    )(
        tile_place.T,
        band_degree.reshape(-1, TILE),
        head_degree.reshape(-1, TILE),
        arrow_reach.reshape(-1, TILE),
        band_feats,
        head_feats,
        mix_weights,
        tile_vals,
        arrow_cols,
        arrow_rows,
    )


def solution(mesh):
    split = Mesh(
        mesh.devices.reshape(NZ, NY, NX, NL, NC), (*ROWS, *FEAT)
    )
    return jax.shard_map(
        body,
        mesh=split,
        in_specs=(
            P(ROWS, FEAT),
            P(ROWS, FEAT),
            P(None, None, FEAT),
            P(ROWS, None),
            P(ROWS, None, None),
            P(ROWS, None),
            P(ROWS),
            P(None, ROWS),
            P(ROWS),
            P(),
        ),
        out_specs=(P(ROWS, FEAT), P(ROWS, FEAT)),
        check_vma=False,
    )
```

time: 87.9 us -> 67 us (0.76)
  Pallas kernels: 82.4 us -> 63.5 us
  local copies, waits for them, and re-layouts: 3.83 us -> 2.47 us
    pallas_call x1, Pallas kernels: 82.4 us -> 63.5 us  [body(): pl.pallas_call(kernel, out_shape=(jax.ShapeDtypeStruct((rows, width), F32...]
    unnamed x7 -> x4, local copies, waits for them, and re-layouts: 3.83 us -> 2.47 us
where the time goes in v2:
time: 67 us; the launch traced here: 66.6 us
  Pallas kernels  63.5 us (95%)
  local copies, waits for them, and re-layouts  2.47 us (4%)
    pallas_call x1, Pallas kernels, body(): pl.pallas_call(kernel, out_shape=(jax.ShapeDtypeStruct((rows, width), F32...  63.5 us
    unnamed x4, local copies, waits for them, and re-layouts  2.47 us

profile of v2, /device:TPU:1, one launch (start us, length us, event | category | flops | bytes accessed | tf_op | source)
XLA Modules:
  0.0 66.6 jit_solution(5632135718063504103)
XLA Ops:
  0.6 63.5 %shard_map.113 = (f32[512,256]{1,0:T(8,128)}, f32[4,256]{1,0:T(4,128)}) custom-call(s32[3,32]{1,0:T(4,128)} %bitcast.4, s32[4,128]{1,0:T(4,128)} %bitcast.5, s32[4,128]{1,0:T(4,128)} %bitcast.6, s32[4,128]{1,0:T(4,128)} %bitcast.7, f32[512,256]{1,0:T(8,128)} %x_hbm.1, f32[4,256]{1,0:T(4,128)} %h_hbm.1, bf16[2,1024,256]{2,1,0:T(8,128)(2,1)} %w_hbm.1, ...), custom_call_target="tpu_custom_call" | custom-call | tf_op jit(solution)/shard_map/pallas_call | solution.py:571
  64.1 0.0 copy-start
  64.1 1.9 %copy.14 = f32[512,256]{1,0:T(8,128)} copy(f32[512,256]{1,0:T(8,128)} %get-tuple-element.4) | data formatting | bytes 1048576
  66.0 0.0 copy-done
  66.0 0.6 copy.15
Async XLA Ops:
  64.1 1.9 %copy-start = (f32[4,256]{1,0:T(4,128)S(1)}, f32[4,256]{1,0:T(4,128)}, u32[]{:S(2)}) copy-start(f32[4,256]{1,0:T(4,128)} %get-tuple-element.5) | copy-start | bytes 12292

commit v3 on v2

--- a/solution.py
+++ b/solution.py
@@ -14,7 +14,7 @@
 ROWS = ("z", "yh", "x")
 FEAT = ("yl", "core")
 TILE = 128
-CHUNKS = 4
+CHUNKS = 8
 
 
 def dot(a, b):
@@ -26,10 +26,10 @@
 
 
 def kernel(
-    place,
-    deg,
-    hdeg,
-    reach,
+    place_hbm,
+    deg_hbm,
+    hdeg_hbm,
+    reach_hbm,
     x_hbm,
     h_hbm,
     w_hbm,
@@ -38,6 +38,10 @@
     r_hbm,
     band_out,
     head_out,
+    place,
+    deg,
+    hdeg,
+    reach,
     xin,
     wts,
     tiles,
@@ -158,6 +162,12 @@
     load_t = load(4, t_hbm, tiles.at[pl.ds(0, t_hbm.shape[0])])
     load_c = load(5, c_hbm, cols)
     load_w1 = load(6, w_hbm.at[1], wts.at[1])
+    load_small = [
+        load(8, place_hbm, place),
+        load(9, deg_hbm, deg),
+        load(10, hdeg_hbm, hdeg),
+        load(11, reach_hbm, reach),
+    ]
     gath[0, pl.ds(me_f, 1)] = xin[...].astype(BF16)[None]
     load_h.wait()
     others = [has_left, has_right, greet_up, greet_down]
@@ -452,6 +462,8 @@
     own0, over0 = gather_start(0, CHUNKS)
     load_r.wait()
     x0 = head_partial(0, rws)
+    for copy in load_small:
+        copy.wait()
     tabled = tables()
     for copy in heads_f:
         copy.wait_recv()
@@ -464,32 +476,39 @@
     load_t.wait()
     tabled.wait()
     build()
-    hand0 = [hand_on(0, over0, 0)]
+    hand0, halo0 = [], []
+
+    def mix_next(step, over, hand, halo):
+        if len(hand) < CHUNKS:
+            hand.append(hand_on(step, over, len(hand)))
+        hand[len(halo)].wait_recv()
+        halo.append(mix(step, len(halo)))
+
+    hand0.append(hand_on(0, over0, 0))
+    own0.wait_recv()
+    mix_next(0, over0, hand0, halo0)
+    mix_next(0, over0, hand0, halo0)
+    mix_next(0, over0, hand0, halo0)
     for copy in heads_x:
         copy.wait_recv()
     along_y, along_z = spread_y(jnp.concatenate([h4[k] for k in range(NX)], axis=0))
-    hand0.append(hand_on(0, over0, 1))
-    own0.wait_recv()
-    hand0[0].wait_recv()
-    halo0 = [mix(0, 0)]
+    mix_next(0, over0, hand0, halo0)
+    mix_next(0, over0, hand0, halo0)
     z0 = x_finish(0, x0)
-    hand0.append(hand_on(0, over0, 2))
-    hand0[1].wait_recv()
-    halo0.append(mix(0, 1))
-    hand0.append(hand_on(0, over0, 3))
-    hand0[2].wait_recv()
+    mix_next(0, over0, hand0, halo0)
     relay_on(halo0[0])
-    halo0.append(mix(0, 2))
-    hand0[3].wait_recv()
-    halo0.append(mix(0, 3))
+    mix_next(0, over0, hand0, halo0)
+    mix_next(0, over0, hand0, halo0)
+    relay_on(halo0[2])
+    edges()
     own_band(0)
-    edges()
+    relay_on(halo0[4])
+    along_z = hand_y(along_y, along_z)
+    relay_on(halo0[6])
+    y0 = z_finish(0, z0)
     load_c.wait()
     for i in range(tile_rows):
         mask_cols(i)
-    y0 = z_finish(0, z0)
-    along_z = hand_y(along_y, along_z)
-    relay_on(halo0[2])
     permute_rows()
     hscale[...] = lax.rsqrt(down_rows(hdeg[pl.ds(x, 1), :].astype(F32)))
     h_scale = hscale[pl.ds(pl.multiple_of(z * piece, piece), piece), :]
@@ -498,32 +517,28 @@
     halo_band(0)
     feat_b = feat_start(0, y_finish(0, y0))
     gath[1, pl.ds(me_f, 1)] = state(0, along_z).astype(BF16)[None]
-    own1, over1 = gather_start(1, 2)
+    own1, over1 = gather_start(1, CHUNKS)
     x1 = head_partial(1, rws_p)
     h1 = jnp.maximum(feat_finish(0, 0, feat_b) * h_scale, 0.0)
     feat_c = feat_start(1, h1)
-    over1 += [over_send(1, 2), over_send(1, 3)]
-    hand1 = [hand_on(1, over1, 0)]
     load_w1.wait()
-    hand1.append(hand_on(1, over1, 1))
+    hand1, halo1 = [hand_on(1, over1, 0)], []
     own1.wait_recv()
-    hand1[0].wait_recv()
-    halo1 = [mix(1, 0)]
+    for _i in range(3):
+        mix_next(1, over1, hand1, halo1)
+    z1 = x_finish(1, x1)
+    for _i in range(3):
+        mix_next(1, over1, hand1, halo1)
+    relay_on(halo1[0])
+    mix_next(1, over1, hand1, halo1)
+    mix_next(1, over1, hand1, halo1)
+    relay_on(halo1[2])
     along_x, along_z = spread_x(feat_finish(1, 1, feat_c))
-    z1 = x_finish(1, x1)
-    hand1.append(hand_on(1, over1, 2))
-    hand1[1].wait_recv()
-    halo1.append(mix(1, 1))
-    hand1.append(hand_on(1, over1, 3))
-    hand1[2].wait_recv()
-    halo1.append(mix(1, 2))
-    hand1[3].wait_recv()
-    halo1.append(mix(1, 3))
-    relay_on(halo1[0])
+    relay_on(halo1[4])
+    own_band(1)
+    y1 = z_finish(1, z1)
+    relay_on(halo1[6])
     along_z = hand_x(along_x, along_z)
-    y1 = z_finish(1, z1)
-    own_band(1)
-    relay_on(halo1[2])
     feat_d = feat_start(2, y_finish(1, y1))
     halo_finish(halo1)
     halo_band(1)
@@ -548,6 +563,17 @@
     halo_sent(halo1)
 
 
+def write_out(band, head, band_out, head_out, sem):
+    copies = [
+        pltpu.make_async_copy(src, dst, sem.at[i])
+        for i, (src, dst) in enumerate(((band, band_out), (head, head_out)))
+    ]
+    for copy in copies:
+        copy.start()
+    for copy in copies:
+        copy.wait()
+
+
 N_COPIES = 240
 
 
@@ -568,15 +594,16 @@
     piece = heads // (NZ * NX)
     vmem = pl.BlockSpec(memory_space=pltpu.VMEM)
     hbm = pl.BlockSpec(memory_space=pl.ANY)
-    return pl.pallas_call(
+    results = pl.pallas_call(
         kernel,
-        out_shape=(
-            jax.ShapeDtypeStruct((rows, width), F32),
-            jax.ShapeDtypeStruct(head_feats.shape, F32),
-        ),
-        in_specs=[vmem] * 4 + [hbm] * 6,
+        out_shape=(pltpu.VMEM((rows, width), F32), pltpu.VMEM(head_feats.shape, F32)),
+        in_specs=[hbm] * 10,
         out_specs=(vmem, vmem),
         scratch_shapes=[
+            pltpu.VMEM(tile_place.shape[::-1], jnp.int32),
+            pltpu.VMEM((rows // TILE, TILE), jnp.int32),
+            pltpu.VMEM((heads // TILE, TILE), jnp.int32),
+            pltpu.VMEM((rows // TILE, TILE), jnp.int32),
             pltpu.VMEM((rows, width), F32),
             pltpu.VMEM(mix_weights.shape, BF16),
             pltpu.VMEM((tile_vals.shape[0] + 1, TILE, TILE), BF16),
@@ -597,13 +624,13 @@
             pltpu.VMEM((3, NL * NC, piece, width), BF16),
             pltpu.VMEM((NL * NC, *head_feats.shape), F32),
             pltpu.VMEM((NX, *head_feats.shape), F32),
-            pltpu.VMEM((2, 2, rows // CHUNKS, width), BF16),
+            pltpu.VMEM((2, CHUNKS // 2, rows // CHUNKS, width), BF16),
             pltpu.VMEM((2, NZ, NX, piece, width), BF16),
             pltpu.VMEM((heads // NX, TILE), F32),
             pltpu.VMEM((rows, TILE), F32),
             pltpu.VMEM((8, TILE), jnp.int32),
             pltpu.SMEM((8, TILE), jnp.int32),
-            pltpu.SemaphoreType.DMA((8,)),
+            pltpu.SemaphoreType.DMA((12,)),
             pltpu.SemaphoreType.DMA((N_COPIES,)),
             pltpu.SemaphoreType.DMA((N_COPIES,)),
         ],
@@ -620,6 +647,16 @@
         arrow_cols,
         arrow_rows,
     )
+    return pl.pallas_call(
+        write_out,
+        out_shape=(
+            jax.ShapeDtypeStruct((rows, width), F32),
+            jax.ShapeDtypeStruct(head_feats.shape, F32),
+        ),
+        in_specs=[vmem, vmem],
+        out_specs=(hbm, hbm),
+        scratch_shapes=[pltpu.SemaphoreType.DMA((2,))],
+    )(*(pltpu.with_memory_space_constraint(r, pltpu.VMEM) for r in results))
 
 
 def solution(mesh):

time: 67 us -> 63.1 us (0.942)
  local copies, waits for them, and re-layouts: 2.47 us -> 0 us
  Pallas kernels: 63.5 us -> 62.3 us
    unnamed x4 -> x0, local copies, waits for them, and re-layouts: 2.47 us -> none
    pallas_call x1 -> x2, Pallas kernels: 63.5 us -> 62.3 us  [the longest x1 61.5 us: body(): pl.pallas_call(kernel, out_shape=(pltpu.VMEM((rows, width), F32), pltpu.V...]
where the time goes in v3:
time: 63.1 us; the launch traced here: 63 us
  Pallas kernels  62.3 us (99%)
  between operations  0.64 us (1%)
    pallas_call x1, Pallas kernels, body(): pl.pallas_call(kernel, out_shape=(pltpu.VMEM((rows, width), F32), pltpu.V...  61.5 us

profile of v3, /device:TPU:1, one launch (start us, length us, event | category | flops | bytes accessed | tf_op | source)
XLA Modules:
  0.0 63.0 jit_solution(6992675986672930275)
XLA Ops:
  0.6 61.5 %shard_map.113 = (f32[512,256]{1,0:T(8,128)S(1)}, f32[4,256]{1,0:T(4,128)S(1)}) custom-call(s32[3,32]{1,0:T(4,128)} %bitcast.4, s32[4,128]{1,0:T(4,128)} %bitcast.5, s32[4,128]{1,0:T(4,128)} %bitcast.6, s32[4,128]{1,0:T(4,128)} %bitcast.7, f32[512,256]{1,0:T(8,128)} %x_hbm.1, f32[4,256]{1,0:T(4,128)} %h_hbm.1, bf16[2,1024,256]{2,1,0:T(8,128)(2,1)} %w_hbm.1, ...), custom_call_target="tpu_custom_call" | custom-call | tf_op jit(solution)/shard_map/pallas_call | solution.py:597
  62.2 0.8 %shard_map.114 = (f32[512,256]{1,0:T(8,128)}, f32[4,256]{1,0:T(4,128)}) custom-call(f32[512,256]{1,0:T(8,128)S(1)} %get-tuple-element.4.band, f32[4,256]{1,0:T(4,128)S(1)} %get-tuple-element.5.head), custom_call_target="tpu_custom_call" | custom-call | tf_op jit(solution)/shard_map/pallas_call | solution.py:650

commit v4 on v3

--- a/solution.py
+++ b/solution.py
@@ -15,6 +15,8 @@
 FEAT = ("yl", "core")
 TILE = 128
 CHUNKS = 8
+RELAYED = (0, 1, 2, 4)
+VIA = (6, 7)
 
 
 def dot(a, b):
@@ -59,11 +61,18 @@
     zrcv,
     ysrc,
     yrcv,
+    yout,
+    yown,
+    hf_last,
     feat_h,
     hf,
     h4,
     relay,
+    through,
     head,
+    half4,
+    half_b,
+    cols_p,
     hscale,
     bscale,
     lines,
@@ -101,35 +110,57 @@
     down = at_rank(jnp.maximum(rank - NX, 0))
     at_first, at_last = {"x": 0 * x}, {"x": 0 * x + last_x}
     corner = jnp.logical_or(first_col, last_col)
+    inner = jnp.logical_not(corner)
+    beside = {"x": x + 1 - 2 * (x % 2)}
+    beyond = {"x": x + 1 - 2 * (x % 2), "yl": 1 - yl}
     greet_up, greet_down = jnp.logical_and(corner, above), jnp.logical_and(corner, below)
     mate = {"core": 1 - core}
     across = {"yl": 1 - yl}
     f_peers = [across, {"yl": 1 - yl, "core": 1 - core}, mate]
     far_slot = (1 - yl) * NC + core
 
-    used = [0]
-    started = []
-
-    def remote(src, dst, device):
-        i = used[0]
-        used[0] += 1
+    n_send, n_recv, ends = [0], [0], []
+
+    def fresh(count):
+        count[0] += 1
+        return count[0] - 1
+
+    def copy_of(src, dst, device, s, r):
         return pltpu.make_async_remote_copy(
             src_ref=src,
             dst_ref=dst,
-            send_sem=ssem.at[i],
-            recv_sem=rsem.at[i],
+            send_sem=ssem.at[s],
+            recv_sem=rsem.at[r],
             device_id=device,
             device_id_type=MESH,
         )
 
-    def push(src, dst, device):
-        copy = remote(src, dst, device)
+    def whole_of(like, s, r):
+        return copy_of(like, like, mate, s, r)
+
+    def group(like, copies):
+        s, r = fresh(n_send), fresh(n_recv)
+        for src, dst, device in copies:
+            copy_of(src, dst, device, s, r).start()
+        whole = whole_of(like, s, r)
+        ends.append(whole)
+        return [whole]
+
+    def push(src, dst, device, s):
+        copy = copy_of(src, dst, device, s, fresh(n_recv))
         copy.start()
-        started.append(copy)
         return copy
 
+    shared = {}
+
+    def shared_send(name, step, like):
+        if (name, step) not in shared:
+            shared[name, step] = fresh(n_send)
+            ends.append(whole_of(like, shared[name, step], 0))
+        return shared[name, step]
+
     barrier = pltpu.get_barrier_semaphore()
-    greet = [*z_peers.values(), *y_peers.values(), *x_peers.values(), *f_peers]
+    greet = [*z_peers.values(), *y_peers.values(), *x_peers.values(), *f_peers, beyond]
     for peer in greet:
         pl.semaphore_signal(barrier, inc=1, device_id=peer, device_id_type=MESH)
 
@@ -178,9 +209,10 @@
     def head_partial(step, weights):
         part[...] = dot(weights[...], gath[step, me_f]).reshape(part.shape)
         part_b[step] = part[...].astype(BF16)
-        return [
-            push(part_b.at[step, (x + k) % NX], xrcv.at[step, k - 1], x_peers[k]) for k in x_order
-        ]
+        return group(
+            xrcv.at[step],
+            [(part_b.at[step, (x + k) % NX], xrcv.at[step, k - 1], x_peers[k]) for k in x_order],
+        )
 
     def x_finish(step, copies):
         total = part[x]
@@ -189,9 +221,10 @@
         for k in range(1, NX):
             total = total + xrcv[step, k - 1].astype(F32)
         zsrc[step] = total.reshape(NZ, -1, total.shape[-1]).astype(BF16)
-        return [
-            push(zsrc.at[step, (z + k) % NZ], zrcv.at[step, k - 1], z_peers[k]) for k in z_order
-        ]
+        return group(
+            zrcv.at[step],
+            [(zsrc.at[step, (z + k) % NZ], zrcv.at[step, k - 1], z_peers[k]) for k in z_order],
+        )
 
     def z_finish(step, copies):
         for copy in copies:
@@ -199,20 +232,44 @@
         total = zsrc[step, z].astype(F32)
         for k in range(1, NZ):
             total = total + zrcv[step, k - 1].astype(F32)
-        ysrc[step] = total
-        return [push(ysrc.at[step], yrcv.at[step, k - 1], y_peers[k]) for k in y_order]
+        if step:
+            per = head_out.shape[0]
+            for k in range(NY):
+                yout[k] = total[k * per : (k + 1) * per]
+            return group(
+                yown, [(yout.at[(yh + k) % NY], yown.at[k - 1], y_peers[k]) for k in y_order]
+            )
+        ysrc[...] = total.astype(BF16)
+        return group(yrcv, [(ysrc, yrcv.at[k - 1], y_peers[k]) for k in y_order])
 
     def y_finish(step, copies):
         for copy in copies:
             copy.wait_recv()
-        total = ysrc[step]
-        for k in range(1, NY):
-            total = total + yrcv[step, k - 1]
-        return total
+        if step:
+            return yout[yh] + sum(yown[k] for k in range(NY - 1))
+        return ysrc[...].astype(F32) + sum(yrcv[k].astype(F32) for k in range(NY - 1))
+
+    def last_start(value):
+        hf_last[me_f] = value
+        return spread_f(hf_last)
+
+    def spread_f(ref):
+        return group(
+            ref.at[pl.ds(0, len(f_peers))], [(ref.at[me_f], ref.at[me_f], peer) for peer in f_peers]
+        )
+
+    def last_finish(copies):
+        for copy in copies:
+            copy.wait_recv()
+        width = hf_last.shape[-1]
+        return sum(
+            dot(hf_last[f].astype(BF16), wts[1, f * width : (f + 1) * width, :])
+            for f in range(NL * NC)
+        )
 
     def feat_start(i, value):
         feat_h[i, pl.ds(me_f, 1)] = value.astype(BF16)[None]
-        return [push(feat_h.at[i, me_f], feat_h.at[i, me_f], peer) for peer in f_peers]
+        return spread_f(feat_h.at[i])
 
     def feat_finish(i, step, copies):
         for copy in copies:
@@ -222,19 +279,54 @@
             dot(feat_h[i, f], wts[step, f * width : (f + 1) * width, :]) for f in range(NL * NC)
         )
 
+    vias = []
+    via_s, via_r = fresh(n_send), fresh(n_recv)
+    all_vias = whole_of(through, via_s, via_r)
+
     def over_send(step, i):
         part_of = gath.at[step, me_f, pl.ds(i * step_rows, step_rows)]
-        return push(part_of, part_of, across)
+        s = shared_send("over", step, gath.at[step, 0])
+        if step or i not in VIA:
+            return push(part_of, part_of, across, s)
+        spare = through.at[VIA.index(i)]
+        r = fresh(n_recv)
+        straight = copy_of(part_of, part_of, across, s, r)
+        beside_copy = copy_of(part_of, spare, beside, s, via_r)
+        vias.append(copy_of(spare, part_of, beyond, via_s, r))
+
+        @pl.when(corner)
+        def _():
+            beside_copy.start()
+
+        @pl.when(inner)
+        def _():
+            straight.start()
+
+        return straight
+
+    def cross_on():
+        @pl.when(inner)
+        def _():
+            all_vias.wait_recv()
+            for onward in vias:
+                onward.start()
+
+    def via_sent():
+        @pl.when(inner)
+        def _():
+            all_vias.wait_send()
 
     def gather_start(step, ahead):
         over = [over_send(step, i) for i in range(ahead)]
-        own = push(gath.at[step, me_f], gath.at[step, me_f], mate)
-        return own, over
+        mine = gath.at[step, me_f]
+        return group(mine, [(mine, mine, mate)])[0], over
 
     def hand_on(step, over, i):
         over[i].wait_recv()
         came = gath.at[step, far_slot, pl.ds(i * step_rows, step_rows)]
-        return push(came, came, mate)
+        return push(came, came, mate, shared_send("hand", step, gath.at[step, 0]))
+
+    halo_sems = [[fresh(n_send) for _i in range(3)] + [fresh(n_recv) for _i in range(2)] for _j in range(2)]
 
     def mix(step, i):
         width = gath.shape[-1]
@@ -247,9 +339,10 @@
         src = win.at[step, pl.ds(rows + i * step_rows, step_rows)]
         to_left_part = win.at[step, pl.ds(i * step_rows, step_rows)]
         to_right_part = win.at[step, pl.ds(2 * rows + i * step_rows, step_rows)]
-        to_right = remote(src, to_left_part, right)
-        to_left = remote(src, to_right_part, left)
-        if i % 2:
+        s_right, s_left, s_pass, r_right, r_left = halo_sems[step]
+        to_right = copy_of(src, to_left_part, right, s_right, r_right)
+        to_left = copy_of(src, to_right_part, left, s_left, r_left)
+        if i not in RELAYED:
 
             @pl.when(has_right)
             def _():
@@ -261,12 +354,12 @@
 
             return to_right, to_left, None
 
-        spare = relay.at[step, i // 2]
-        by_first, by_last = remote(src, spare, at_first), remote(src, spare, at_last)
-        used[0] -= 4
-        pass_right = remote(spare, to_left_part, up)
-        pass_left = remote(spare, to_right_part, down)
-        used[0] += 2
+        spare = relay.at[step, RELAYED.index(i)]
+        r_spare = fresh(n_recv)
+        by_first = copy_of(src, spare, at_first, s_right, r_spare)
+        by_last = copy_of(src, spare, at_last, s_left, r_spare)
+        pass_right = copy_of(spare, to_left_part, up, s_pass, r_right)
+        pass_left = copy_of(spare, to_right_part, down, s_pass, r_left)
 
         @pl.when(relay_right)
         def _():
@@ -299,92 +392,123 @@
             by_last.wait_recv()
             pass_left.start()
 
-    def halo_finish(halos):
+    def halo_whole(step):
+        s_right, s_left, s_pass, r_right, r_left = halo_sems[step]
+        block = win.at[step, pl.ds(0, rows)]
+        return (
+            whole_of(block, s_right, r_right),
+            whole_of(block, s_left, r_left),
+            whole_of(relay.at[step], s_pass, r_left),
+        )
+
+    def halo_finish(step):
+        rightward, leftward, _unused = halo_whole(step)
+
         @pl.when(has_left)
         def _():
-            for copies in halos:
-                copies[0].wait_recv()
+            rightward.wait_recv()
 
         @pl.when(has_right)
         def _():
-            for copies in halos:
-                copies[1].wait_recv()
-
-    def halo_sent(halos):
-        for copies in halos:
-            if copies[2] is None:
-
-                @pl.when(has_right)
-                def _():
-                    copies[0].wait_send()
-
-                @pl.when(has_left)
-                def _():
-                    copies[1].wait_send()
-
-                continue
-            by_first, by_last, pass_right, pass_left = copies[2]
-
-            @pl.when(relay_right)
-            def _():
-                by_first.wait_send()
-
-            @pl.when(relay_left)
-            def _():
-                by_last.wait_send()
-
-            @pl.when(serve_right)
-            def _():
-                pass_right.wait_send()
-
-            @pl.when(serve_left)
-            def _():
-                pass_left.wait_send()
-
-            @pl.when(jnp.logical_and(has_right, jnp.logical_not(last_col)))
-            def _():
-                copies[0].wait_send()
-
-            @pl.when(jnp.logical_and(has_left, jnp.logical_not(first_col)))
-            def _():
-                copies[1].wait_send()
+            leftward.wait_recv()
+
+    def halo_sent(step):
+        rightward, leftward, passed = halo_whole(step)
+
+        @pl.when(has_right)
+        def _():
+            rightward.wait_send()
+
+        @pl.when(has_left)
+        def _():
+            leftward.wait_send()
+
+        @pl.when(jnp.logical_or(serve_right, serve_left))
+        def _():
+            passed.wait_send()
 
     piece = head.shape[-2]
+    half = head.shape[-1]
+
+    z_sems = [(fresh(n_send), fresh(n_recv)) for _i in range(2)]
+
+    def all_z(step):
+        return whole_of(head.at[step, pl.ds(0, NZ - 1)], *z_sems[step])
+
+    def hand_z(step, src):
+        for k in z_order:
+            copy_of(src, src, z_peers[k], *z_sems[step]).start()
 
     def spread(step, src, peers):
-        def to_z(piece_ref):
-            return [push(piece_ref, piece_ref, z_peers[k]) for k in z_order]
-
-        return {k: push(src, src, peer) for k, peer in peers.items()}, to_z(src)
+        s = shared_send("head", step, head.at[step, 0, pl.ds(0, len(peers))])
+        along = {k: push(src, src, peer, s) for k, peer in peers.items()}
+        hand_z(step, src)
+        return along
 
     def spread_y(value):
         head[0, z, yh] = value.astype(BF16)
         return spread(0, head.at[0, z, yh], y_peers)
 
-    def hand_y(along_y, along_z):
+    def hand_y(along_y):
         for k in (1, 3, 2):
             along_y[k].wait_recv()
-            src = head.at[0, z, (yh + NY - k) % NY]
-            along_z = along_z + [push(src, src, z_peers[q]) for q in z_order]
-        return along_z
+            hand_z(0, head.at[0, z, (yh + NY - k) % NY])
+
+    def second_y(copies):
+        for copy in copies:
+            copy.wait_recv()
+        lines = jnp.concatenate([half4[i] for i in range(NZ)], axis=0)
+        per = lines.shape[0]
+        at = pl.ds(pl.multiple_of(yh * per, per), per)
+        half_b[0, x, at] = lines.astype(BF16)
+        src = half_b.at[0, x, at]
+        return group(
+            half_b.at[0, 0, pl.ds(0, (NY - 1) * per)], [(src, src, y_peers[k]) for k in y_order]
+        )
+
+    def second_x(step, copies):
+        for copy in copies:
+            copy.wait_recv()
+        src = half_b.at[step, x]
+        return group(half_b.at[step, pl.ds(0, NX - 1)], [(src, src, x_peers[k]) for k in x_order])
 
     def spread_x(value):
-        head[1, z, x] = value.astype(BF16)
-        return spread(1, head.at[1, z, x], x_peers)
-
-    def hand_x(along_x, along_z):
+        head[1, z, x] = value[:, :half].astype(BF16)
+        at = pl.ds(pl.multiple_of(z * piece, piece), piece)
+        half_b[1, x, at] = value[:, half:].astype(BF16)
+        src = half_b.at[1, x, at]
+        second = group(
+            half_b.at[1, 0, pl.ds(0, (NZ - 1) * piece)], [(src, src, z_peers[k]) for k in z_order]
+        )
+        return spread(1, head.at[1, z, x], x_peers), second
+
+    def hand_x(along_x):
         for k in (1, 3, 2):
             along_x[k].wait_recv()
-            src = head.at[1, z, (x + NX - k) % NX]
-            along_z = along_z + [push(src, src, z_peers[q]) for q in z_order]
-        return along_z
-
-    def head_finish(step, along_z):
-        for copy in along_z:
+            hand_z(1, head.at[1, z, (x + NX - k) % NX])
+
+    def head_band(step, along_x):
+        all_z(step).wait_recv()
+        if step:
+            first = jnp.concatenate([head[1, :, k].reshape(-1, half) for k in range(NX)])
+        else:
+            first = head[0].reshape(-1, half)
+        one = dot(cols[...], first)
+        for copy in along_x:
             copy.wait_recv()
-        if step:
-            return jnp.concatenate([head[1, :, k].reshape(-1, head.shape[-1]) for k in range(NX)])
-        return head[0].reshape(-1, head.shape[-1])
+        by = cols if step else cols_p
+        two = dot(by[...], half_b[step].reshape(-1, half))
+        return jnp.concatenate([one, two], axis=1)
+
+    def permute_cols():
+        per = head_out.shape[0]
+        for g in range(NX):
+            shape = (cols.shape[1], part.shape[1])
+            come = lax.broadcasted_iota(jnp.int32, shape, 0)
+            to = lax.broadcasted_iota(jnp.int32, shape, 1)
+            row = (to // per) % NZ * (NY * NX * per) + to // (NZ * per) * (NX * per)
+            pick = jnp.where(come == row + g * per + to % per, 1.0, 0.0).astype(BF16)
+            cols_p[:, g * shape[1] : (g + 1) * shape[1]] = dot(cols[...], pick).astype(BF16)
 
     n_tiles = place.shape[1]
     n_cols = 3 * tile_rows
@@ -453,12 +577,12 @@
             dense[:, 2 * rows :], win[step, 2 * rows :, :]
         )
 
-    def state(step, along):
-        whole = head_finish(step, along)
+    def state(step, along_x):
+        from_head = head_band(step, along_x)
         scale = jnp.concatenate([bscale[...], bscale[...]], axis=1)
-        return jnp.maximum((acc[...] + dot(cols[...], whole)) * scale, 0.0)
-
-    heads_f = [push(hf.at[me_f], hf.at[me_f], peer) for peer in f_peers]
+        return jnp.maximum((acc[...] + from_head) * scale, 0.0)
+
+    heads_f = spread_f(hf)
     own0, over0 = gather_start(0, CHUNKS)
     load_r.wait()
     x0 = head_partial(0, rws)
@@ -469,13 +593,15 @@
         copy.wait_recv()
     load_w0.wait()
     width = hf.shape[-1]
-    h4[x] = sum(
+    own_rows = sum(
         dot(hf[f].astype(BF16), wts[0, f * width : (f + 1) * width, :]) for f in range(NL * NC)
     )
-    heads_x = [push(h4.at[x], h4.at[x], x_peers[k]) for k in x_order]
-    load_t.wait()
-    tabled.wait()
-    build()
+    h4[x] = own_rows[:, :half]
+    half4[z] = own_rows[:, half:]
+    heads_x = group(h4.at[pl.ds(0, NX - 1)], [(h4.at[x], h4.at[x], x_peers[k]) for k in x_order])
+    second = group(
+        half4.at[pl.ds(0, NZ - 1)], [(half4.at[z], half4.at[z], z_peers[k]) for k in z_order]
+    )
     hand0, halo0 = [], []
 
     def mix_next(step, over, hand, halo):
@@ -484,6 +610,7 @@
         hand[len(halo)].wait_recv()
         halo.append(mix(step, len(halo)))
 
+    cross_on()
     hand0.append(hand_on(0, over0, 0))
     own0.wait_recv()
     mix_next(0, over0, hand0, halo0)
@@ -491,76 +618,85 @@
     mix_next(0, over0, hand0, halo0)
     for copy in heads_x:
         copy.wait_recv()
-    along_y, along_z = spread_y(jnp.concatenate([h4[k] for k in range(NX)], axis=0))
+    along_y = spread_y(jnp.concatenate([h4[k] for k in range(NX)], axis=0))
     mix_next(0, over0, hand0, halo0)
     mix_next(0, over0, hand0, halo0)
     z0 = x_finish(0, x0)
-    mix_next(0, over0, hand0, halo0)
     relay_on(halo0[0])
     mix_next(0, over0, hand0, halo0)
+    relay_on(halo0[1])
+    second = second_y(second)
     mix_next(0, over0, hand0, halo0)
     relay_on(halo0[2])
+    mix_next(0, over0, hand0, halo0)
+    load_t.wait()
+    tabled.wait()
+    build()
+    relay_on(halo0[4])
+    hand_y(along_y)
     edges()
     own_band(0)
-    relay_on(halo0[4])
-    along_z = hand_y(along_y, along_z)
-    relay_on(halo0[6])
+    second = second_x(0, second)
     y0 = z_finish(0, z0)
     load_c.wait()
     for i in range(tile_rows):
         mask_cols(i)
+    permute_cols()
     permute_rows()
     hscale[...] = lax.rsqrt(down_rows(hdeg[pl.ds(x, 1), :].astype(F32)))
     h_scale = hscale[pl.ds(pl.multiple_of(z * piece, piece), piece), :]
     h_scale = jnp.concatenate([h_scale, h_scale], axis=1)
-    halo_finish(halo0)
+    halo_finish(0)
     halo_band(0)
+    gath[1, pl.ds(me_f, 1)] = state(0, second).astype(BF16)[None]
     feat_b = feat_start(0, y_finish(0, y0))
-    gath[1, pl.ds(me_f, 1)] = state(0, along_z).astype(BF16)[None]
     own1, over1 = gather_start(1, CHUNKS)
     x1 = head_partial(1, rws_p)
-    h1 = jnp.maximum(feat_finish(0, 0, feat_b) * h_scale, 0.0)
-    feat_c = feat_start(1, h1)
     load_w1.wait()
     hand1, halo1 = [hand_on(1, over1, 0)], []
     own1.wait_recv()
-    for _i in range(3):
+    for _i in range(2):
+        mix_next(1, over1, hand1, halo1)
+    h1 = jnp.maximum(feat_finish(0, 0, feat_b) * h_scale, 0.0)
+    feat_c = feat_start(1, h1)
+    for _i in range(2):
         mix_next(1, over1, hand1, halo1)
     z1 = x_finish(1, x1)
-    for _i in range(3):
-        mix_next(1, over1, hand1, halo1)
+    mix_next(1, over1, hand1, halo1)
     relay_on(halo1[0])
     mix_next(1, over1, hand1, halo1)
+    relay_on(halo1[1])
     mix_next(1, over1, hand1, halo1)
     relay_on(halo1[2])
-    along_x, along_z = spread_x(feat_finish(1, 1, feat_c))
+    mix_next(1, over1, hand1, halo1)
+    along_x, second = spread_x(feat_finish(1, 1, feat_c))
     relay_on(halo1[4])
+    y1 = z_finish(1, z1)
+    hand_x(along_x)
     own_band(1)
-    y1 = z_finish(1, z1)
-    relay_on(halo1[6])
-    along_z = hand_x(along_x, along_z)
-    feat_d = feat_start(2, y_finish(1, y1))
-    halo_finish(halo1)
+    second = second_x(1, second)
+    feat_d = last_start(y_finish(1, y1))
+    halo_finish(1)
     halo_band(1)
-    band_out[...] = state(1, along_z)
-    sums = feat_finish(2, 1, feat_d)
+    band_out[...] = state(1, second)
+    sums = last_finish(feat_d)
     per = head_out.shape[0]
     near_z = hscale.shape[0] // (per * NX * NY)
     hscale[...] = lax.rsqrt(down_rows(hdeg[pl.ds(z // near_z, 1), :].astype(F32)))
     at = pl.multiple_of((z % near_z) * NY * NX * per + yh * NX * per, NX * per)
     near = hscale[pl.ds(at, NX * per), :]
     near = jnp.concatenate([near, near], axis=1)
-    mine, own_scale = jnp.zeros(head_out.shape, F32), jnp.zeros(head_out.shape, F32)
-    for k in range(NY):
-        mine = mine + jnp.where(yh == k, sums[k * per : (k + 1) * per, :], 0.0)
+    own_scale = jnp.zeros(head_out.shape, F32)
     for k in range(NX):
         own_scale = own_scale + jnp.where(x == k, near[k * per : (k + 1) * per, :], 0.0)
-    head_out[...] = jnp.maximum(mine * own_scale, 0.0)
-
-    for copy in started:
-        copy.wait_send()
-    halo_sent(halo0)
-    halo_sent(halo1)
+    head_out[...] = jnp.maximum(sums * own_scale, 0.0)
+
+    for whole in ends + [all_z(0), all_z(1)]:
+        whole.wait_send()
+    via_sent()
+    halo_sent(0)
+    halo_sent(1)
+    assert (n_send[0], n_recv[0]) == (N_SEND, N_RECV), (n_send, n_recv)
 
 
 def write_out(band, head, band_out, head_out, sem):
@@ -574,7 +710,7 @@
         copy.wait()
 
 
-N_COPIES = 240
+N_SEND, N_RECV = 33, 71
 
 
 def body(
@@ -619,20 +755,27 @@
             pltpu.VMEM((2, NX - 1, heads // NX, width), BF16),
             pltpu.VMEM((2, NZ, piece, width), BF16),
             pltpu.VMEM((2, NZ - 1, piece, width), BF16),
-            pltpu.VMEM((2, piece, width), F32),
-            pltpu.VMEM((2, NY - 1, piece, width), F32),
-            pltpu.VMEM((3, NL * NC, piece, width), BF16),
+            pltpu.VMEM((piece, width), BF16),
+            pltpu.VMEM((NY - 1, piece, width), BF16),
+            pltpu.VMEM((NY, *head_feats.shape), F32),
+            pltpu.VMEM((NY - 1, *head_feats.shape), F32),
             pltpu.VMEM((NL * NC, *head_feats.shape), F32),
-            pltpu.VMEM((NX, *head_feats.shape), F32),
-            pltpu.VMEM((2, CHUNKS // 2, rows // CHUNKS, width), BF16),
-            pltpu.VMEM((2, NZ, NX, piece, width), BF16),
+            pltpu.VMEM((2, NL * NC, piece, width), BF16),
+            pltpu.VMEM((NL * NC, *head_feats.shape), F32),
+            pltpu.VMEM((NX, head_feats.shape[0], width // 2), F32),
+            pltpu.VMEM((2, len(RELAYED), rows // CHUNKS, width), BF16),
+            pltpu.VMEM((len(VIA), rows // CHUNKS, width), BF16),
+            pltpu.VMEM((2, NZ, NX, piece, width // 2), BF16),
+            pltpu.VMEM((NZ, head_feats.shape[0], width // 2), F32),
+            pltpu.VMEM((2, NX, heads // NX, width // 2), BF16),
+            pltpu.VMEM(arrow_cols.shape, BF16),
             pltpu.VMEM((heads // NX, TILE), F32),
             pltpu.VMEM((rows, TILE), F32),
             pltpu.VMEM((8, TILE), jnp.int32),
             pltpu.SMEM((8, TILE), jnp.int32),
             pltpu.SemaphoreType.DMA((12,)),
-            pltpu.SemaphoreType.DMA((N_COPIES,)),
-            pltpu.SemaphoreType.DMA((N_COPIES,)),
+            pltpu.SemaphoreType.DMA((N_SEND,)),
+            pltpu.SemaphoreType.DMA((N_RECV,)),
         ],
         compiler_params=pltpu.CompilerParams(collective_id=0, has_side_effects=True),
     )(

time: 63.1 us -> 59.3 us (0.940)
  Pallas kernels: 62.3 us -> 58.5 us
    pallas_call x1, Pallas kernels: 61.5 us -> 57.7 us  [body(): pl.pallas_call(kernel, out_shape=(pltpu.VMEM((rows, width), F32), pltpu.V...]
where the time goes in v4:
time: 59.3 us; the launch traced here: 59.1 us
  Pallas kernels  58.5 us (99%)
  between operations  0.64 us (1%)
    pallas_call x1, Pallas kernels, body(): pl.pallas_call(kernel, out_shape=(pltpu.VMEM((rows, width), F32), pltpu.V...  57.7 us

profile of v4, /device:TPU:1, one launch (start us, length us, event | category | flops | bytes accessed | tf_op | source)
XLA Modules:
  0.0 59.1 jit_solution(7142831918742893434)
XLA Ops:
  0.6 57.7 %shard_map.113 = (f32[512,256]{1,0:T(8,128)S(1)}, f32[4,256]{1,0:T(4,128)S(1)}) custom-call(s32[3,32]{1,0:T(4,128)} %bitcast.4, s32[4,128]{1,0:T(4,128)} %bitcast.5, s32[4,128]{1,0:T(4,128)} %bitcast.6, s32[4,128]{1,0:T(4,128)} %bitcast.7, f32[512,256]{1,0:T(8,128)} %x_hbm.1, f32[4,256]{1,0:T(4,128)} %h_hbm.1, bf16[2,1024,256]{2,1,0:T(8,128)(2,1)} %w_hbm.1, ...), custom_call_target="tpu_custom_call" | custom-call | tf_op jit(solution)/shard_map/pallas_call | solution.py:733
  58.3 0.8 %shard_map.114 = (f32[512,256]{1,0:T(8,128)}, f32[4,256]{1,0:T(4,128)}) custom-call(f32[512,256]{1,0:T(8,128)S(1)} %get-tuple-element.4.band, f32[4,256]{1,0:T(4,128)S(1)} %get-tuple-element.5.head), custom_call_target="tpu_custom_call" | custom-call | tf_op jit(solution)/shard_map/pallas_call | solution.py:793

commit v5 on v4

--- a/solution.py
+++ b/solution.py
@@ -621,11 +621,11 @@
     along_y = spread_y(jnp.concatenate([h4[k] for k in range(NX)], axis=0))
     mix_next(0, over0, hand0, halo0)
     mix_next(0, over0, hand0, halo0)
+    second = second_y(second)
     z0 = x_finish(0, x0)
     relay_on(halo0[0])
     mix_next(0, over0, hand0, halo0)
     relay_on(halo0[1])
-    second = second_y(second)
     mix_next(0, over0, hand0, halo0)
     relay_on(halo0[2])
     mix_next(0, over0, hand0, halo0)
@@ -655,26 +655,25 @@
     load_w1.wait()
     hand1, halo1 = [hand_on(1, over1, 0)], []
     own1.wait_recv()
-    for _i in range(2):
-        mix_next(1, over1, hand1, halo1)
+    mix_next(1, over1, hand1, halo1)
     h1 = jnp.maximum(feat_finish(0, 0, feat_b) * h_scale, 0.0)
     feat_c = feat_start(1, h1)
-    for _i in range(2):
+    mix_next(1, over1, hand1, halo1)
+    z1 = x_finish(1, x1)
+    for _i in range(3):
         mix_next(1, over1, hand1, halo1)
-    z1 = x_finish(1, x1)
+    along_x, second = spread_x(feat_finish(1, 1, feat_c))
     mix_next(1, over1, hand1, halo1)
     relay_on(halo1[0])
     mix_next(1, over1, hand1, halo1)
     relay_on(halo1[1])
     mix_next(1, over1, hand1, halo1)
     relay_on(halo1[2])
-    mix_next(1, over1, hand1, halo1)
-    along_x, second = spread_x(feat_finish(1, 1, feat_c))
+    hand_x(along_x)
+    y1 = z_finish(1, z1)
     relay_on(halo1[4])
-    y1 = z_finish(1, z1)
-    hand_x(along_x)
+    second = second_x(1, second)
     own_band(1)
-    second = second_x(1, second)
     feat_d = last_start(y_finish(1, y1))
     halo_finish(1)
     halo_band(1)

time: 59.3 us -> 57.3 us (0.966)
  Pallas kernels: 58.5 us -> 56.6 us
    pallas_call x1, Pallas kernels: 57.7 us -> 55.7 us  [body(): pl.pallas_call(kernel, out_shape=(pltpu.VMEM((rows, width), F32), pltpu.V...]
where the time goes in v5:
time: 57.3 us; the launch traced here: 57.2 us
  Pallas kernels  56.6 us (99%)
  between operations  0.64 us (1%)
    pallas_call x1, Pallas kernels, body(): pl.pallas_call(kernel, out_shape=(pltpu.VMEM((rows, width), F32), pltpu.V...  55.7 us

profile of v5, /device:TPU:1, one launch (start us, length us, event | category | flops | bytes accessed | tf_op | source)
XLA Modules:
  0.0 57.2 jit_solution(9739608221730277927)
XLA Ops:
  0.6 55.7 %shard_map.113 = (f32[512,256]{1,0:T(8,128)S(1)}, f32[4,256]{1,0:T(4,128)S(1)}) custom-call(s32[3,32]{1,0:T(4,128)} %bitcast.4, s32[4,128]{1,0:T(4,128)} %bitcast.5, s32[4,128]{1,0:T(4,128)} %bitcast.6, s32[4,128]{1,0:T(4,128)} %bitcast.7, f32[512,256]{1,0:T(8,128)} %x_hbm.1, f32[4,256]{1,0:T(4,128)} %h_hbm.1, bf16[2,1024,256]{2,1,0:T(8,128)(2,1)} %w_hbm.1, ...), custom_call_target="tpu_custom_call" | custom-call | tf_op jit(solution)/shard_map/pallas_call | solution.py:732
  56.4 0.8 %shard_map.114 = (f32[512,256]{1,0:T(8,128)}, f32[4,256]{1,0:T(4,128)}) custom-call(f32[512,256]{1,0:T(8,128)S(1)} %get-tuple-element.4.band, f32[4,256]{1,0:T(4,128)S(1)} %get-tuple-element.5.head), custom_call_target="tpu_custom_call" | custom-call | tf_op jit(solution)/shard_map/pallas_call | solution.py:792

commit v6 on v5

--- a/solution.py
+++ b/solution.py
@@ -159,6 +159,19 @@
             ends.append(whole_of(like, shared[name, step], 0))
         return shared[name, step]
 
+    def load(i, src, dst):
+        copy = pltpu.make_async_copy(src, dst, lsem.at[i])
+        copy.start()
+        return copy
+
+    quarter = rows // 4
+    loads_x = []
+    for q in range(4):
+        at = pl.ds(q * quarter, quarter)
+        loads_x.append(load(12 + q, x_hbm.at[at], xin.at[at]))
+    load_h = load(1, h_hbm, hf.at[me_f])
+    load_r = load(2, r_hbm, rws)
+
     barrier = pltpu.get_barrier_semaphore()
     greet = [*z_peers.values(), *y_peers.values(), *x_peers.values(), *f_peers, beyond]
     for peer in greet:
@@ -180,15 +193,10 @@
     def _():
         pl.semaphore_signal(barrier, inc=1, device_id=down, device_id_type=MESH)
 
-    def load(i, src, dst):
-        copy = pltpu.make_async_copy(src, dst, lsem.at[i])
-        copy.start()
-        return copy
-
-    load_x = load(0, x_hbm, xin)
-    load_h = load(1, h_hbm, hf.at[me_f])
-    load_r = load(2, r_hbm, rws)
-    load_x.wait()
+    for q, copy in enumerate(loads_x):
+        copy.wait()
+        at = slice(q * quarter, (q + 1) * quarter)
+        gath[0, pl.ds(me_f, 1), at] = xin[at].astype(BF16)[None]
     load_w0 = load(3, w_hbm.at[0], wts.at[0])
     load_t = load(4, t_hbm, tiles.at[pl.ds(0, t_hbm.shape[0])])
     load_c = load(5, c_hbm, cols)
@@ -199,7 +207,6 @@
         load(10, hdeg_hbm, hdeg),
         load(11, reach_hbm, reach),
     ]
-    gath[0, pl.ds(me_f, 1)] = xin[...].astype(BF16)[None]
     load_h.wait()
     others = [has_left, has_right, greet_up, greet_down]
     pl.semaphore_wait(
@@ -401,14 +408,15 @@
             whole_of(relay.at[step], s_pass, r_left),
         )
 
-    def halo_finish(step):
+    def halo_finish(step, side):
         rightward, leftward, _unused = halo_whole(step)
-
-        @pl.when(has_left)
+        from_left = first_col if side else jnp.logical_not(first_col)
+
+        @pl.when(jnp.logical_and(has_left, from_left))
         def _():
             rightward.wait_recv()
 
-        @pl.when(has_right)
+        @pl.when(jnp.logical_and(has_right, jnp.logical_not(from_left)))
         def _():
             leftward.wait_recv()
 
@@ -493,12 +501,13 @@
             first = jnp.concatenate([head[1, :, k].reshape(-1, half) for k in range(NX)])
         else:
             first = head[0].reshape(-1, half)
-        one = dot(cols[...], first)
+        one = None if step else dot(cols[...], first)
         for copy in along_x:
             copy.wait_recv()
-        by = cols if step else cols_p
-        two = dot(by[...], half_b[step].reshape(-1, half))
-        return jnp.concatenate([one, two], axis=1)
+        other = half_b[step].reshape(-1, half)
+        if step:
+            return dot(cols[...], jnp.concatenate([first, other], axis=1))
+        return jnp.concatenate([one, dot(cols_p[...], other)], axis=1)
 
     def permute_cols():
         per = head_out.shape[0]
@@ -572,15 +581,16 @@
     def own_band(step):
         acc[...] = dot(dense[:, rows : 2 * rows], win[step, rows : 2 * rows, :])
 
-    def halo_band(step):
-        acc[...] += dot(dense[:, :rows], win[step, :rows, :]) + dot(
-            dense[:, 2 * rows :], win[step, 2 * rows :, :]
-        )
+    def halo_side(step, side):
+        halo_finish(step, side)
+        first = jnp.where(first_col, 2 * rows * (1 - side), 2 * rows * side)
+        at = pl.ds(pl.multiple_of(first, rows), rows)
+        return dot(dense[:, at], win[step, at, :])
 
     def state(step, along_x):
-        from_head = head_band(step, along_x)
+        acc[...] += head_band(step, along_x)
         scale = jnp.concatenate([bscale[...], bscale[...]], axis=1)
-        return jnp.maximum((acc[...] + from_head) * scale, 0.0)
+        return jnp.maximum((acc[...] + halo_side(step, 1)) * scale, 0.0)
 
     heads_f = spread_f(hf)
     own0, over0 = gather_start(0, CHUNKS)
@@ -646,8 +656,7 @@
     hscale[...] = lax.rsqrt(down_rows(hdeg[pl.ds(x, 1), :].astype(F32)))
     h_scale = hscale[pl.ds(pl.multiple_of(z * piece, piece), piece), :]
     h_scale = jnp.concatenate([h_scale, h_scale], axis=1)
-    halo_finish(0)
-    halo_band(0)
+    acc[...] += halo_side(0, 0)
     gath[1, pl.ds(me_f, 1)] = state(0, second).astype(BF16)[None]
     feat_b = feat_start(0, y_finish(0, y0))
     own1, over1 = gather_start(1, CHUNKS)
@@ -669,14 +678,13 @@
     relay_on(halo1[1])
     mix_next(1, over1, hand1, halo1)
     relay_on(halo1[2])
+    y1 = z_finish(1, z1)
     hand_x(along_x)
-    y1 = z_finish(1, z1)
     relay_on(halo1[4])
     second = second_x(1, second)
     own_band(1)
+    acc[...] += halo_side(1, 0)
     feat_d = last_start(y_finish(1, y1))
-    halo_finish(1)
-    halo_band(1)
     band_out[...] = state(1, second)
     sums = last_finish(feat_d)
     per = head_out.shape[0]
@@ -772,7 +780,7 @@
             pltpu.VMEM((rows, TILE), F32),
             pltpu.VMEM((8, TILE), jnp.int32),
             pltpu.SMEM((8, TILE), jnp.int32),
-            pltpu.SemaphoreType.DMA((12,)),
+            pltpu.SemaphoreType.DMA((16,)),
             pltpu.SemaphoreType.DMA((N_SEND,)),
             pltpu.SemaphoreType.DMA((N_RECV,)),
         ],

time: 57.3 us -> 56.5 us (0.986)
  Pallas kernels: 56.6 us -> 55.7 us
    pallas_call x1, Pallas kernels: 55.7 us -> 54.9 us  [body(): pl.pallas_call(kernel, out_shape=(pltpu.VMEM((rows, width), F32), pltpu.V...]
where the time goes in v6:
time: 56.5 us; the launch traced here: 56.3 us
  Pallas kernels  55.7 us (99%)
  between operations  0.64 us (1%)
    pallas_call x1, Pallas kernels, body(): pl.pallas_call(kernel, out_shape=(pltpu.VMEM((rows, width), F32), pltpu.V...  54.9 us

profile of v6, /device:TPU:1, one launch (start us, length us, event | category | flops | bytes accessed | tf_op | source)
XLA Modules:
  0.0 56.3 jit_solution(18186711250727196559)
XLA Ops:
  0.6 54.9 %shard_map.113 = (f32[512,256]{1,0:T(8,128)S(1)}, f32[4,256]{1,0:T(4,128)S(1)}) custom-call(s32[3,32]{1,0:T(4,128)} %bitcast.4, s32[4,128]{1,0:T(4,128)} %bitcast.5, s32[4,128]{1,0:T(4,128)} %bitcast.6, s32[4,128]{1,0:T(4,128)} %bitcast.7, f32[512,256]{1,0:T(8,128)} %x_hbm.1, f32[4,256]{1,0:T(4,128)} %h_hbm.1, bf16[2,1024,256]{2,1,0:T(8,128)(2,1)} %w_hbm.1, ...), custom_call_target="tpu_custom_call" | custom-call | tf_op jit(solution)/shard_map/pallas_call | solution.py:740
  55.5 0.8 %shard_map.114 = (f32[512,256]{1,0:T(8,128)}, f32[4,256]{1,0:T(4,128)}) custom-call(f32[512,256]{1,0:T(8,128)S(1)} %get-tuple-element.4.band, f32[4,256]{1,0:T(4,128)S(1)} %get-tuple-element.5.head), custom_call_target="tpu_custom_call" | custom-call | tf_op jit(solution)/shard_map/pallas_call | solution.py:800

commit v7 on v6

--- a/solution.py
+++ b/solution.py
@@ -679,8 +679,8 @@
     mix_next(1, over1, hand1, halo1)
     relay_on(halo1[2])
     y1 = z_finish(1, z1)
+    relay_on(halo1[4])
     hand_x(along_x)
-    relay_on(halo1[4])
     second = second_x(1, second)
     own_band(1)
     acc[...] += halo_side(1, 0)

time: 56.5 us -> 56.6 us (level)
  no operation moved by 1% of the time
where the time goes in v7:
time: 56.6 us; the launch traced here: 56.3 us
  Pallas kernels  55.7 us (98%)
  between operations  0.64 us (1%)
    pallas_call x1, Pallas kernels, body(): pl.pallas_call(kernel, out_shape=(pltpu.VMEM((rows, width), F32), pltpu.V...  54.9 us

profile of v7, /device:TPU:1, one launch (start us, length us, event | category | flops | bytes accessed | tf_op | source)
XLA Modules:
  0.0 56.3 jit_solution(11585508419928539168)
XLA Ops:
  0.6 54.9 %shard_map.113 = (f32[512,256]{1,0:T(8,128)S(1)}, f32[4,256]{1,0:T(4,128)S(1)}) custom-call(s32[3,32]{1,0:T(4,128)} %bitcast.4, s32[4,128]{1,0:T(4,128)} %bitcast.5, s32[4,128]{1,0:T(4,128)} %bitcast.6, s32[4,128]{1,0:T(4,128)} %bitcast.7, f32[512,256]{1,0:T(8,128)} %x_hbm.1, f32[4,256]{1,0:T(4,128)} %h_hbm.1, bf16[2,1024,256]{2,1,0:T(8,128)(2,1)} %w_hbm.1, ...), custom_call_target="tpu_custom_call" | custom-call | tf_op jit(solution)/shard_map/pallas_call | solution.py:740
  55.5 0.8 %shard_map.114 = (f32[512,256]{1,0:T(8,128)}, f32[4,256]{1,0:T(4,128)}) custom-call(f32[512,256]{1,0:T(8,128)S(1)} %get-tuple-element.4.band, f32[4,256]{1,0:T(4,128)S(1)} %get-tuple-element.5.head), custom_call_target="tpu_custom_call" | custom-call | tf_op jit(solution)/shard_map/pallas_call | solution.py:800
